TPU v7x, 32 devices: a whole 2x2x4 slice. The times are simulated.
32 devices in a mesh: rep: 4 (over y, x), fsdp: 8 (over z, core).
Axes of the slice: x: 2, y: 2, z: 4, core: 2. Of those that a mesh axis runs over, the one named last changes fastest.
Arguments:
- tokens: bfloat16 [8192, 1280], P(('rep', 'fsdp')), may hold values from -6 to 6
- cotangent: bfloat16 [8192, 1280], P(('rep', 'fsdp')), may hold values from -6 to 6
- lengths: int32 [16], replicated, may hold values from 1 to 1024, 8192 in all
- sequence_order: int32 [16], replicated, may hold values from 0 to 15, each once
- expert_choice: int32 [8192, 7], P(('rep', 'fsdp')), may hold values from 0 to 15, all different within a row; in each aligned block of 256 rows (0 to 255, 256 to 511, ...) at most 224 rows name the same one
- expert_home: int32 [16], replicated, may hold values from 0 to 15, each once
- first_gain: bfloat16 [1280], P('fsdp'), may hold values from 0.5 to 1.5
- w_query: bfloat16 [1280, 1280], P('fsdp'), may hold values from -0.15625 to 0.15625
- w_key: bfloat16 [1280, 1280], P('fsdp'), may hold values from -0.15625 to 0.15625
- w_value: bfloat16 [1280, 1280], P('fsdp'), may hold values from -0.15625 to 0.15625
- w_out: bfloat16 [1280, 1280], P('fsdp'), may hold values from -1 to 1
- second_gain: bfloat16 [1280], P('fsdp'), may hold values from 0.5 to 1.5
- w_router: bfloat16 [1280, 16], P('fsdp'), may hold values from -0.083984375 to 0.083984375
- shared_gate: bfloat16 [1280, 896], P('fsdp'), may hold values from -0.15625 to 0.15625
- shared_up: bfloat16 [1280, 896], P('fsdp'), may hold values from -0.15625 to 0.15625
- shared_down: bfloat16 [896, 1280], P('fsdp'), may hold values from -0.25 to 0.25
- expert_gate: bfloat16 [16, 1280, 896], P('fsdp'), may hold values from -0.15625 to 0.15625
- expert_up: bfloat16 [16, 1280, 896], P('fsdp'), may hold values from -0.15625 to 0.15625
- expert_down: bfloat16 [16, 896, 1280], P('fsdp'), may hold values from -0.75 to 0.75
Outputs:
- output: bfloat16 [8192, 1280], P(('rep', 'fsdp'))
- input_grad: bfloat16 [8192, 1280], P(('rep', 'fsdp'))
- first_gain_grad: float32 [1280], P('fsdp')
- w_query_grad: float32 [1280, 1280], P('fsdp')
- w_key_grad: float32 [1280, 1280], P('fsdp')
- w_value_grad: float32 [1280, 1280], P('fsdp')
- w_out_grad: float32 [1280, 1280], P('fsdp')
- second_gain_grad: float32 [1280], P('fsdp')
- w_router_grad: float32 [1280, 16], P('fsdp')
- shared_gate_grad: float32 [1280, 896], P('fsdp')
- shared_up_grad: float32 [1280, 896], P('fsdp')
- shared_down_grad: float32 [896, 1280], P('fsdp')
- expert_gate_grad: float32 [16, 1280, 896], P('fsdp')
- expert_up_grad: float32 [16, 1280, 896], P('fsdp')
- expert_down_grad: float32 [16, 896, 1280], P('fsdp')
Inputs may be any that keep to these rules, and one draw needn't show every extreme that they name: The lengths add up to 8192, and the longest is exactly 1024. `sequence_order`: a permutation of the 16 sequences. `expert_choice`: each token names 7 different experts; of the 256 tokens of one device at most 224 name any one expert, and on some device some expert is named by exactly 224 of them. `expert_home`: a permutation of the 16 weight slots.
All inputs are finite; a program needn't handle non-finite values.
Results may differ from a plain program's by a relative error of at most 0.023.
Values may be sent and summed in bfloat16 or wider, within the bound.
A program may use at most 320 MiB of HBM per device.

v0:
```python
import math

import jax
import jax.numpy as jnp
from jax import lax
from jax.sharding import PartitionSpec as P

DH = 128
SEQ_MAX = 1024


EPSILON = 1e-06
NEGATIVE = -1e30


def shifted(block, axis, distance):
    devices = range(lax.axis_size(axis))
    route = [(i - distance, i) for i in devices if i - distance in devices]
    return lax.ppermute(block, axis, route)


def rms_scale(values):
    return lax.rsqrt(jnp.mean(values * values, axis=1, keepdims=True) + EPSILON)


def silu_value(values):
    return values / (1.0 + jnp.exp(-values))


def rotary_tables(position, head_size):
    half_size = head_size // 2
    frequency = 1.0 / 10000.0 ** (jnp.arange(half_size, dtype=jnp.float32) / half_size)
    angles = position.astype(jnp.float32)[:, None] * frequency[None, :]
    cosine_table = jnp.cos(angles)
    sine_table = jnp.sin(angles)
    cosine_table = jnp.concatenate([cosine_table, cosine_table], axis=1)[:, None, :]
    sine_table = jnp.concatenate([sine_table, sine_table], axis=1)[:, None, :]
    return (cosine_table, sine_table)


def rotate(values, cosine_table, sine_table):
    half_size = values.shape[-1] // 2
    turned = jnp.concatenate([-values[..., half_size:], values[..., :half_size]], axis=-1)
    return values * cosine_table + turned * sine_table


def rotate_back(values, cosine_table, sine_table):
    half_size = values.shape[-1] // 2
    scaled = values * sine_table
    turned = jnp.concatenate([scaled[..., half_size:], -scaled[..., :half_size]], axis=-1)
    return values * cosine_table + turned


def norm_back(grad_rows, values, scale_rows, gain_vector):
    weighted = grad_rows * gain_vector[None, :]
    gain_grad = jnp.sum(grad_rows * values * scale_rows, axis=0)
    inner_mean = jnp.mean(weighted * values, axis=1, keepdims=True)
    return (
        scale_rows * weighted - values * (scale_rows * scale_rows * scale_rows) * inner_mean,
        gain_grad,
    )


def sequence_starts(lengths, sequence_order, token_index):
    seq_count = lengths.shape[0]
    picker = sequence_order[:, None] == jnp.arange(seq_count, dtype=jnp.int32)[None, :]
    ordered = jnp.sum(jnp.where(picker, lengths[None, :], 0), axis=1)
    opening = jnp.cumsum(ordered) - ordered
    chosen_open = jnp.where(opening[None, :] <= token_index[:, None], opening[None, :], 0)
    return jnp.max(chosen_open, axis=1)


def project(left, right):
    return jnp.dot(left, right, preferred_element_type=jnp.float32)


def per_device(
    tokens,
    cotangent,
    lengths,
    sequence_order,
    expert_choice,
    expert_home,
    first_gain,
    w_query,
    w_key,
    w_value,
    w_out,
    second_gain,
    w_router,
    shared_gate,
    shared_up,
    shared_down,
    expert_gate,
    expert_up,
    expert_down,
):
    tok_rows, width = tokens.shape
    top_count = expert_choice.shape[1]
    experts = expert_home.shape[0]
    local_experts = expert_gate.shape[0]
    groups = lax.axis_size("fsdp")
    capacity = 2 * tok_rows * top_count // experts
    att_width = w_query.shape[1]
    heads = att_width // DH
    reach = (SEQ_MAX + tok_rows - 2) // tok_rows
    window = (reach + 1) * tok_rows
    inv_root = 1.0 / math.sqrt(DH)
    device = lax.axis_index("rep") * groups + lax.axis_index("fsdp")
    token_index = device * tok_rows + jnp.arange(tok_rows, dtype=jnp.int32)
    key_index = (device - reach) * tok_rows + jnp.arange(window, dtype=jnp.int32)
    start_query = sequence_starts(lengths, sequence_order, token_index)
    visible = (
        (key_index[None, :] <= token_index[:, None]) & (key_index[None, :] >= start_query[:, None])
    )[None, :, :]
    cosine_table, sine_table = rotary_tables(token_index - start_query, DH)
    gathered = (
        lax.all_gather(first_gain, "fsdp", axis=0, tiled=True),
        lax.all_gather(w_query, "fsdp", axis=0, tiled=True),
        lax.all_gather(w_key, "fsdp", axis=0, tiled=True),
        lax.all_gather(w_value, "fsdp", axis=0, tiled=True),
        lax.all_gather(w_out, "fsdp", axis=0, tiled=True),
        lax.all_gather(second_gain, "fsdp", axis=0, tiled=True),
        lax.all_gather(w_router, "fsdp", axis=0, tiled=True),
        lax.all_gather(shared_gate, "fsdp", axis=0, tiled=True),
        lax.all_gather(shared_up, "fsdp", axis=0, tiled=True),
        lax.all_gather(shared_down, "fsdp", axis=0, tiled=True),
    )
    (
        attention_norm_gain,
        query_full,
        key_full,
        value_full,
        out_full,
        feedforward_norm_gain,
        router_full,
        sgate_full,
        sup_full,
        sdown_full,
    ) = gathered
    layer_input = tokens.astype(jnp.float32)
    scale_one = rms_scale(layer_input)
    normed_one = (
        layer_input * scale_one * attention_norm_gain.astype(jnp.float32)[None, :]
    ).astype(jnp.bfloat16)
    query_raw = project(normed_one, query_full).reshape(tok_rows, heads, DH)
    key_raw = project(normed_one, key_full).reshape(tok_rows, heads, DH)
    value_raw = project(normed_one, value_full)
    query_rot = rotate(query_raw, cosine_table, sine_table).astype(jnp.bfloat16)
    key_flat = (
        rotate(key_raw, cosine_table, sine_table).astype(jnp.bfloat16).reshape(tok_rows, att_width)
    )
    value_flat = value_raw.astype(jnp.bfloat16)
    key_parts = [key_flat]
    value_parts = [value_flat]
    for distance in range(1, reach + 1):
        moved_key, moved_value = shifted((key_flat, value_flat), ("rep", "fsdp"), distance)
        key_parts.insert(0, moved_key)
        value_parts.insert(0, moved_value)
    keys_window = jnp.concatenate(key_parts, axis=0).reshape(window, heads, DH)
    values_window = jnp.concatenate(value_parts, axis=0).reshape(window, heads, DH)
    scores = (
        jnp.einsum("qhd,khd->hqk", query_rot, keys_window, preferred_element_type=jnp.float32)
        * inv_root
    )
    masked = jnp.where(visible, scores, NEGATIVE)
    top_score = jnp.max(masked, axis=2, keepdims=True)
    expanded = jnp.exp(masked - top_score)
    denominator = jnp.sum(expanded, axis=2, keepdims=True)
    log_total = top_score + jnp.log(denominator)
    probs_low = (expanded / denominator).astype(jnp.bfloat16)
    mixed_rows = jnp.einsum(
        "hqk,khd->qhd", probs_low, values_window, preferred_element_type=jnp.float32
    )
    attended = mixed_rows.astype(jnp.bfloat16).reshape(tok_rows, att_width)
    resid_one = layer_input + project(attended, out_full)
    scale_two = rms_scale(resid_one)
    normed_two = (
        resid_one * scale_two * feedforward_norm_gain.astype(jnp.float32)[None, :]
    ).astype(jnp.bfloat16)
    logits = project(normed_two, router_full)
    choice_hit = expert_choice[:, :, None] == jnp.arange(experts, dtype=jnp.int32)[None, None, :]
    chosen_logits = jnp.sum(jnp.where(choice_hit, logits[:, None, :], 0.0), axis=2)
    gates = jax.nn.softmax(chosen_logits, axis=1)
    slot_choice = jnp.sum(jnp.where(choice_hit, expert_home[None, None, :], 0), axis=2).reshape(-1)
    slot_hit = (slot_choice[:, None] == jnp.arange(experts, dtype=jnp.int32)[None, :]).astype(
        jnp.int32
    )
    placing = jnp.sum((jnp.cumsum(slot_hit, axis=0) - 1) * slot_hit, axis=1)
    destination = slot_choice * capacity + placing
    send_rows = (
        jnp.zeros((experts * capacity, width), jnp.bfloat16)
        .at[destination]
        .set(jnp.repeat(normed_two, top_count, axis=0))
    )
    send_rows = send_rows.reshape(groups, local_experts, capacity, width)
    rows_in = lax.all_to_all(send_rows, "fsdp", split_axis=0, concat_axis=0, tiled=True)
    gate_rows = jnp.einsum(
        "sjcd,jdf->sjcf", rows_in, expert_gate, preferred_element_type=jnp.float32
    )
    up_rows = jnp.einsum("sjcd,jdf->sjcf", rows_in, expert_up, preferred_element_type=jnp.float32)
    hidden_rows = (silu_value(gate_rows) * up_rows).astype(jnp.bfloat16)
    out_rows = jnp.einsum(
        "sjcf,jfd->sjcd", hidden_rows, expert_down, preferred_element_type=jnp.float32
    ).astype(jnp.bfloat16)
    kept_rows, gate_pre, up_pre, out_rows = (rows_in, gate_rows, up_rows, out_rows)
    returned = lax.all_to_all(out_rows, "fsdp", split_axis=0, concat_axis=0, tiled=True).reshape(
        experts * capacity, width
    )
    routed_rows = returned[destination].reshape(tok_rows, top_count, width).astype(jnp.float32)
    expert_output_sum = jnp.sum(gates[:, :, None] * routed_rows, axis=1)
    shared_pre_gate = project(normed_two, sgate_full)
    shared_pre_up = project(normed_two, sup_full)
    shared_hidden = (silu_value(shared_pre_gate) * shared_pre_up).astype(jnp.bfloat16)
    final_rows = resid_one + project(shared_hidden, sdown_full) + expert_output_sum
    output = final_rows.astype(jnp.bfloat16)
    cotan = cotangent.astype(jnp.float32)
    gate_grad = jnp.sum(cotan[:, None, :] * routed_rows, axis=2)
    row_cot = (
        (gates[:, :, None] * cotan[:, None, :])
        .astype(jnp.bfloat16)
        .reshape(tok_rows * top_count, width)
    )
    send_grads = jnp.zeros((experts * capacity, width), jnp.bfloat16).at[destination].set(row_cot)
    send_grads = send_grads.reshape(groups, local_experts, capacity, width)
    back_weights = (
        lax.all_gather(first_gain, "fsdp", axis=0, tiled=True),
        lax.all_gather(w_query, "fsdp", axis=0, tiled=True),
        lax.all_gather(w_key, "fsdp", axis=0, tiled=True),
        lax.all_gather(w_value, "fsdp", axis=0, tiled=True),
        lax.all_gather(w_out, "fsdp", axis=0, tiled=True),
        lax.all_gather(second_gain, "fsdp", axis=0, tiled=True),
        lax.all_gather(w_router, "fsdp", axis=0, tiled=True),
        lax.all_gather(shared_gate, "fsdp", axis=0, tiled=True),
        lax.all_gather(shared_up, "fsdp", axis=0, tiled=True),
        lax.all_gather(shared_down, "fsdp", axis=0, tiled=True),
    )
    again_keys = [key_flat]
    again_values = [value_flat]
    for distance in range(1, reach + 1):
        moved_key, moved_value = shifted((key_flat, value_flat), ("rep", "fsdp"), distance)
        again_keys.insert(0, moved_key)
        again_values.insert(0, moved_value)
    back_keys = jnp.concatenate(again_keys, axis=0).reshape(window, heads, DH)
    back_values = jnp.concatenate(again_values, axis=0).reshape(window, heads, DH)
    rows_back, received_grads = (
        lax.all_to_all(send_rows, "fsdp", split_axis=0, concat_axis=0, tiled=True),
        lax.all_to_all(send_grads, "fsdp", split_axis=0, concat_axis=0, tiled=True),
    )
    gate_back = jnp.einsum(
        "sjcd,jdf->sjcf", rows_back, expert_gate, preferred_element_type=jnp.float32
    )
    up_back = jnp.einsum("sjcd,jdf->sjcf", rows_back, expert_up, preferred_element_type=jnp.float32)
    (
        gain_one_back,
        query_back,
        key_back,
        value_back,
        out_back,
        gain_two_back,
        router_back,
        sgate_back,
        sup_back,
        sdown_back,
    ) = back_weights
    activated = silu_value(gate_back)
    hidden_back = (activated * up_back).astype(jnp.bfloat16)
    expert_down_term = jnp.einsum(
        "sjcf,sjcd->jfd", hidden_back, received_grads, preferred_element_type=jnp.float32
    )
    hidden_grad = jnp.einsum(
        "sjcd,jfd->sjcf", received_grads, expert_down, preferred_element_type=jnp.float32
    )
    sigmoid_gate = 1.0 / (1.0 + jnp.exp(-gate_back))
    gate_grad_rows = (
        hidden_grad * up_back * sigmoid_gate * (1.0 + gate_back * (1.0 - sigmoid_gate))
    ).astype(jnp.bfloat16)
    up_grad_rows = (hidden_grad * activated).astype(jnp.bfloat16)
    expert_gate_term = jnp.einsum(
        "sjcd,sjcf->jdf", rows_back, gate_grad_rows, preferred_element_type=jnp.float32
    )
    expert_up_term = jnp.einsum(
        "sjcd,sjcf->jdf", rows_back, up_grad_rows, preferred_element_type=jnp.float32
    )
    input_rows = jnp.einsum(
        "sjcf,jdf->sjcd", gate_grad_rows, expert_gate, preferred_element_type=jnp.float32
    )
    input_rows = (
        input_rows
        + jnp.einsum("sjcf,jdf->sjcd", up_grad_rows, expert_up, preferred_element_type=jnp.float32)
    ).astype(jnp.bfloat16)
    returned_grads = lax.all_to_all(
        input_rows, "fsdp", split_axis=0, concat_axis=0, tiled=True
    ).reshape(experts * capacity, width)
    routed_input = jnp.sum(
        returned_grads[destination].reshape(tok_rows, top_count, width).astype(jnp.float32), axis=1
    )
    sdown_term = jnp.einsum(
        "tf,td->fd", shared_hidden, cotangent, preferred_element_type=jnp.float32
    )
    shared_hidden_grad = jnp.einsum(
        "td,fd->tf", cotangent, sdown_back, preferred_element_type=jnp.float32
    )
    shared_sigmoid = 1.0 / (1.0 + jnp.exp(-shared_pre_gate))
    shared_gate_low = (
        shared_hidden_grad
        * shared_pre_up
        * shared_sigmoid
        * (1.0 + shared_pre_gate * (1.0 - shared_sigmoid))
    ).astype(jnp.bfloat16)
    shared_up_low = (shared_hidden_grad * silu_value(shared_pre_gate)).astype(jnp.bfloat16)
    sgate_term = jnp.einsum(
        "td,tf->df", normed_two, shared_gate_low, preferred_element_type=jnp.float32
    )
    sup_term = jnp.einsum(
        "td,tf->df", normed_two, shared_up_low, preferred_element_type=jnp.float32
    )
    gate_mean = jnp.sum(gates * gate_grad, axis=1, keepdims=True)
    chosen_grad = gates * (gate_grad - gate_mean)
    logit_grad = jnp.sum(jnp.where(choice_hit, chosen_grad[:, :, None], 0.0), axis=1).astype(
        jnp.bfloat16
    )
    router_term = jnp.einsum(
        "td,te->de", normed_two, logit_grad, preferred_element_type=jnp.float32
    )
    normed_two_grad = jnp.einsum(
        "tf,df->td", shared_gate_low, sgate_back, preferred_element_type=jnp.float32
    )
    normed_two_grad = normed_two_grad + jnp.einsum(
        "tf,df->td", shared_up_low, sup_back, preferred_element_type=jnp.float32
    )
    normed_two_grad = normed_two_grad + jnp.einsum(
        "te,de->td", logit_grad, router_back, preferred_element_type=jnp.float32
    )
    normed_two_grad = normed_two_grad + routed_input
    resid_part, gain_two_term = norm_back(
        normed_two_grad, resid_one, scale_two, gain_two_back.astype(jnp.float32)
    )
    resid_grad = cotan + resid_part
    out_grad_low = resid_grad.astype(jnp.bfloat16)
    out_term = jnp.einsum("ta,td->ad", attended, out_grad_low, preferred_element_type=jnp.float32)
    attended_grad = (
        jnp.einsum("td,ad->ta", out_grad_low, out_back, preferred_element_type=jnp.float32)
        .astype(jnp.bfloat16)
        .reshape(tok_rows, heads, DH)
    )
    scores_back = (
        jnp.einsum("qhd,khd->hqk", query_rot, back_keys, preferred_element_type=jnp.float32)
        * inv_root
    )
    probs_back = jnp.exp(jnp.where(visible, scores_back, NEGATIVE) - log_total)
    probs_back_low = probs_back.astype(jnp.bfloat16)
    probs_grad = jnp.einsum(
        "qhd,khd->hqk", attended_grad, back_values, preferred_element_type=jnp.float32
    )
    inner_sum = jnp.sum(probs_back * probs_grad, axis=2, keepdims=True)
    scores_grad = (probs_back * (probs_grad - inner_sum)).astype(jnp.bfloat16)
    query_grad_rot = (
        jnp.einsum("hqk,khd->qhd", scores_grad, back_keys, preferred_element_type=jnp.float32)
        * inv_root
    )
    key_grad_flat = (
        jnp.einsum("hqk,qhd->khd", scores_grad, query_rot, preferred_element_type=jnp.float32)
        * inv_root
    ).reshape(window, att_width)
    value_grad_flat = jnp.einsum(
        "hqk,qhd->khd", probs_back_low, attended_grad, preferred_element_type=jnp.float32
    ).reshape(window, att_width)
    own_key = key_grad_flat[reach * tok_rows :]
    own_value = value_grad_flat[reach * tok_rows :]
    for distance in range(1, reach + 1):
        lower = (reach - distance) * tok_rows
        incoming_key, incoming_value = (
            shifted(
                key_grad_flat[lower : lower + tok_rows].astype(jnp.bfloat16),
                ("rep", "fsdp"),
                -distance,
            ).astype(jnp.float32),
            shifted(
                value_grad_flat[lower : lower + tok_rows].astype(jnp.bfloat16),
                ("rep", "fsdp"),
                -distance,
            ).astype(jnp.float32),
        )
        own_key = own_key + incoming_key
        own_value = own_value + incoming_value
    query_grad = (
        rotate_back(query_grad_rot, cosine_table, sine_table)
        .astype(jnp.bfloat16)
        .reshape(tok_rows, att_width)
    )
    key_grad = (
        rotate_back(own_key.reshape(tok_rows, heads, DH), cosine_table, sine_table)
        .astype(jnp.bfloat16)
        .reshape(tok_rows, att_width)
    )
    value_grad = own_value.astype(jnp.bfloat16)
    query_term = jnp.einsum("td,ta->da", normed_one, query_grad, preferred_element_type=jnp.float32)
    key_term = jnp.einsum("td,ta->da", normed_one, key_grad, preferred_element_type=jnp.float32)
    value_term = jnp.einsum("td,ta->da", normed_one, value_grad, preferred_element_type=jnp.float32)
    normed_one_grad = jnp.einsum(
        "ta,da->td", query_grad, query_back, preferred_element_type=jnp.float32
    )
    normed_one_grad = normed_one_grad + jnp.einsum(
        "ta,da->td", key_grad, key_back, preferred_element_type=jnp.float32
    )
    normed_one_grad = normed_one_grad + jnp.einsum(
        "ta,da->td", value_grad, value_back, preferred_element_type=jnp.float32
    )
    input_part, gain_one_term = norm_back(
        normed_one_grad, layer_input, scale_one, gain_one_back.astype(jnp.float32)
    )
    input_grad = (resid_grad + input_part).astype(jnp.bfloat16)
    shares = (
        lax.psum_scatter(
            gain_one_term.astype(jnp.bfloat16), "fsdp", scatter_dimension=0, tiled=True
        ).astype(jnp.float32),
        lax.psum_scatter(
            query_term.astype(jnp.bfloat16), "fsdp", scatter_dimension=0, tiled=True
        ).astype(jnp.float32),
        lax.psum_scatter(
            key_term.astype(jnp.bfloat16), "fsdp", scatter_dimension=0, tiled=True
        ).astype(jnp.float32),
        lax.psum_scatter(
            value_term.astype(jnp.bfloat16), "fsdp", scatter_dimension=0, tiled=True
        ).astype(jnp.float32),
        lax.psum_scatter(
            out_term.astype(jnp.bfloat16), "fsdp", scatter_dimension=0, tiled=True
        ).astype(jnp.float32),
        lax.psum_scatter(
            gain_two_term.astype(jnp.bfloat16), "fsdp", scatter_dimension=0, tiled=True
        ).astype(jnp.float32),
        lax.psum_scatter(
            router_term.astype(jnp.bfloat16), "fsdp", scatter_dimension=0, tiled=True
        ).astype(jnp.float32),
        lax.psum_scatter(
            sgate_term.astype(jnp.bfloat16), "fsdp", scatter_dimension=0, tiled=True
        ).astype(jnp.float32),
        lax.psum_scatter(
            sup_term.astype(jnp.bfloat16), "fsdp", scatter_dimension=0, tiled=True
        ).astype(jnp.float32),
        lax.psum_scatter(
            sdown_term.astype(jnp.bfloat16), "fsdp", scatter_dimension=0, tiled=True
        ).astype(jnp.float32),
    )
    summed = (
        lax.psum(shares[0].astype(jnp.bfloat16), "rep").astype(jnp.float32),
        lax.psum(shares[1].astype(jnp.bfloat16), "rep").astype(jnp.float32),
        lax.psum(shares[2].astype(jnp.bfloat16), "rep").astype(jnp.float32),
        lax.psum(shares[3].astype(jnp.bfloat16), "rep").astype(jnp.float32),
        lax.psum(shares[4].astype(jnp.bfloat16), "rep").astype(jnp.float32),
        lax.psum(shares[5].astype(jnp.bfloat16), "rep").astype(jnp.float32),
        lax.psum(shares[6].astype(jnp.bfloat16), "rep").astype(jnp.float32),
        lax.psum(shares[7].astype(jnp.bfloat16), "rep").astype(jnp.float32),
        lax.psum(shares[8].astype(jnp.bfloat16), "rep").astype(jnp.float32),
        lax.psum(shares[9].astype(jnp.bfloat16), "rep").astype(jnp.float32),
        lax.psum(expert_gate_term.astype(jnp.bfloat16), "rep").astype(jnp.float32),
        lax.psum(expert_up_term.astype(jnp.bfloat16), "rep").astype(jnp.float32),
        lax.psum(expert_down_term.astype(jnp.bfloat16), "rep").astype(jnp.float32),
    )
    return (
        output,
        input_grad,
        summed[0],
        summed[1],
        summed[2],
        summed[3],
        summed[4],
        summed[5],
        summed[6],
        summed[7],
        summed[8],
        summed[9],
        summed[10],
        summed[11],
        summed[12],
    )


def solution(mesh):
    placed = (
        P(("rep", "fsdp"), None),
        P(("rep", "fsdp"), None),
        P(),
        P(),
        P(("rep", "fsdp"), None),
        P(),
        P("fsdp"),
        P("fsdp", None),
        P("fsdp", None),
        P("fsdp", None),
        P("fsdp", None),
        P("fsdp"),
        P("fsdp", None),
        P("fsdp", None),
        P("fsdp", None),
        P("fsdp", None),
        P("fsdp", None, None),
        P("fsdp", None, None),
        P("fsdp", None, None),
    )
    return jax.shard_map(
        per_device,
        mesh=mesh,
        in_specs=placed,
        out_specs=(
            P(("rep", "fsdp"), None),
            P(("rep", "fsdp"), None),
            P("fsdp"),
            P("fsdp", None),
            P("fsdp", None),
            P("fsdp", None),
            P("fsdp", None),
            P("fsdp"),
            P("fsdp", None),
            P("fsdp", None),
            P("fsdp", None),
            P("fsdp", None),
            P("fsdp", None, None),
            P("fsdp", None, None),
            P("fsdp", None, None),
        ),
        check_vma=False,
    )
```

profile of v0, /device:TPU:0, one launch (start us, length us, event | category | flops | bytes accessed | tf_op | source)
XLA Modules:
  0.0 2141.5 jit_solution(7542020992066891226)
XLA Ops:
  15.7 19.1 all-reduce.5
  37.3 7.3 reduce-window.19
  48.4 3.8 all-gather.13.cloned.1.call-done
  52.2 4.0 fusion.89
  58.9 33.3 %all-gather.11.cloned.1.call-done = bf16[1280,1280]{1,0:T(8,128)(2,1)} async-done(((bf16[160,1280]{1,0:T(8,128)(2,1)}), bf16[1280,1280]{1,0:T(8,128)(2,1)}) %all-gather.11.cloned.1.call-update) | async-done | bytes 3276816 | tf_op jit(solution)/shard_map/all_gather | solution.py:119
  111.4 5.4 collective-permute-start.4
  116.8 94.3 %all-gather.9.cloned.1.call-done = bf16[1280,1280]{1,0:T(8,128)(2,1)} async-done(((bf16[160,1280]{1,0:T(8,128)(2,1)}), bf16[1280,1280]{1,0:T(8,128)(2,1)}) %all-gather.9.cloned.1.call-update) | async-done | bytes 3276816 | tf_op jit(solution)/shard_map/all_gather | solution.py:121
  211.1 3.8 convolution_convert_fusion.9
  219.5 7.1 collective-permute-start.2
  246.7 5.3 collective-permute-done.1
  254.0 26.1 %collective-permute-done.2 = bf16[256,1280]{1,0:T(8,128)(2,1)} collective-permute-done((bf16[256,1280]{1,0:T(8,128)(2,1)}, bf16[256,1280]{1,0:T(8,128)(2,1)}, u32[]{:S(2)}, u32[]{:S(2)}) %collective-permute-start.2) | collective-permute-done | bytes 655392 | tf_op jit(solution)/shard_map/ppermute | solution.py:19
  286.0 5.7 copy.157
  302.4 4.4 fusion.53
  314.4 7.5 reshape.459
  321.9 17.2 scatter_custom_fusion
  339.1 20.0 all-to-all-start
  359.1 206.9 %all-gather = bf16[8,160,16]{1,2,0:T(8,128)(2,1)S(1)} all-gather(bf16[1,160,16]{1,2,0:T(8,128)(2,1)S(1)} %bitcast.245), channel_id=1, replica_groups=mesh['rep'=4,'fsdp'=8] {'fsdp'}, dimensions={0}, use_global_device_ids=true | all-gather | bytes 46080 | tf_op jit(solution)/shard_map/all_gather | solution.py:124
  566.2 4.7 mul.401
  570.9 10.3 mul.406
  583.1 24.4 %scatter_custom_fusion.1 = bf16[3584,1280]{1,0:T(8,128)(2,1)} fusion(s32[1792]{0:T(1024)S(1)} %fusion.83, f32[1792,1280]{1,0:T(8,128)} %mul.406, f32[1792]{0:T(1024)S(1)} %div.72, bf16[]{:T(256)} %constant.60.clone.1), kind=kCustom, calls=%fused_computation.58 | custom fusion | flops 4587520 | bytes 18358274 | tf_op jit(solution)/shard_map/scatter | solution.py:224
  607.5 5.4 all-to-all-start.2
  612.9 16.3 fusion.17
  629.2 14.9 fusion.19
  644.2 169.4 %all-to-all-done.2 = bf16[8,2,224,1280]{3,2,1,0:T(8,128)(2,1)} async-done(((bf16[8,2,224,1280]{3,2,1,0:T(8,128)(2,1)}), bf16[8,2,224,1280]{3,2,1,0:T(8,128)(2,1)}, u32[]{:S(2)}, u32[]{:S(2)}) %all-to-all-start.2) | async-done | bytes 9175072 | tf_op jit(solution)/shard_map/all_to_all | solution.py:248
  813.6 22.2 %fusion.3 = (bf16[8,2,224,896]{3,2,0,1:T(8,128)(2,1)}, bf16[8,2,224,896]{3,2,0,1:T(8,128)(2,1)}, bf16[8,2,224,896]{3,2,0,1:T(8,128)(2,1)S(1)}) fusion(f32[2,8,224,896]{3,2,1,0:T(8,128)} %fusion.19, f32[2,8,224,896]{3,2,1,0:T(8,128)} %fusion.17, bf16[2,896,1280]{2,1,0:T(8,128)(2,1)} %param.37, bf16[8,2,224,1280]{3,2,1,0:T(8,128)(2,1)} %all-to-all-done.2), kind=kOutput, calls=%fused_computation.16 | convolution fusion | flops 8269004800 | bytes 58720256 | tf_op jit(solution)/shard_map/sjcd,jfd->sjcf/dot_general | solution.py:271
  838.4 13.9 fusion.11
  852.3 7.9 copy.181
  860.2 5.0 all-to-all-start.1
  867.2 17.2 fusion.41
  884.3 18.0 fusion.12
  902.3 7.9 copy.186
  910.2 211.1 %all-to-all-done.1 = bf16[8,2,224,1280]{3,2,1,0:T(8,128)(2,1)} async-done(((bf16[8,2,224,1280]{3,2,1,0:T(8,128)(2,1)}), bf16[8,2,224,1280]{3,2,1,0:T(8,128)(2,1)}, u32[]{:S(2)}, u32[]{:S(2)}) %all-to-all-start.1) | async-done | bytes 9175072 | tf_op jit(solution)/shard_map/all_to_all | solution.py:207
  1121.3 5.1 all-to-all-start.3
  1148.3 15.2 gather_fusion
  1163.5 8.1 reshape.437
  1171.6 8.8 multiply_reduce_fusion.1
  1180.5 189.6 %all-to-all-done.3 = bf16[8,2,224,1280]{3,2,1,0:T(8,128)(2,1)} async-done(((bf16[8,2,224,1280]{3,2,1,0:T(8,128)(2,1)}), bf16[8,2,224,1280]{3,2,1,0:T(8,128)(2,1)}, u32[]{:S(2)}, u32[]{:S(2)}) %all-to-all-start.3) | async-done | bytes 9175072 | tf_op jit(solution)/shard_map/all_to_all | solution.py:292
  1370.1 15.0 gather_fusion.1
  1385.1 8.1 reshape.438
  1393.3 7.3 reduce_sum.177
  1408.2 4.4 convolution_convert_fusion.8
  1414.8 11.6 multiply_reduce_fusion
  1427.9 6.6 multiply_convert_fusion
  1434.5 6.7 broadcast_multiply_fusion
  1445.3 6.1 fusion.101
  1457.0 44.1 %collective-permute-done.15 = bf16[256,1280]{0,1:T(8,128)(2,1)S(1)} collective-permute-done((bf16[256,1280]{0,1:T(8,128)(2,1)S(1)}, bf16[256,1280]{0,1:T(8,128)(2,1)S(1)}, u32[]{:S(2)}, u32[]{:S(2)}) %collective-permute-start.15) | collective-permute-done | bytes 655392 | tf_op jit(solution)/shard_map/ppermute | solution.py:19
  1501.1 4.2 collective-permute-done.14
  1505.3 21.0 collective-permute-done.13
  1529.7 4.0 fusion.100
  1539.5 56.1 %collective-permute-done.11 = bf16[256,1280]{0,1:T(8,128)(2,1)S(1)} collective-permute-done((bf16[256,1280]{0,1:T(8,128)(2,1)S(1)}, bf16[256,1280]{0,1:T(8,128)(2,1)S(1)}, u32[]{:S(2)}, u32[]{:S(2)}) %collective-permute-start.11) | collective-permute-done | bytes 655392 | tf_op jit(solution)/shard_map/ppermute | solution.py:19
  1595.6 8.8 collective-permute-done.9
  1609.0 16.1 bitcast_convert_fusion
  1625.1 15.6 bitcast_convert_fusion.1
  1642.1 15.7 bitcast_convert_fusion.2
  1657.8 64.4 %reduce-scatter.15.cloned.1.call-done = bf16[160,1280]{1,0:T(8,128)(2,1)} async-done(((bf16[1280,1280]{1,0:T(8,128)(2,1)}), bf16[160,1280]{1,0:T(8,128)(2,1)}) %reduce-scatter.15.cloned.1.call-update) | async-done | bytes 409616 | tf_op jit(solution)/shard_map/reduce_scatter | solution.py:424
  1722.2 42.5 %reduce-scatter.13.cloned.1.call-done = bf16[160,1280]{1,0:T(8,128)(2,1)} async-done(((bf16[1280,1280]{1,0:T(8,128)(2,1)}), bf16[160,1280]{1,0:T(8,128)(2,1)}) %reduce-scatter.13.cloned.1.call-update) | async-done | bytes 409616 | tf_op jit(solution)/shard_map/reduce_scatter | solution.py:421
  1765.5 4.4 fusion.106
  1771.7 25.1 %reduce-scatter.25.cloned.1.call-done = bf16[160,16]{1,0:T(8,128)(2,1)} async-done(((bf16[1280,16]{1,0:T(8,128)(2,1)}), bf16[160,16]{1,0:T(8,128)(2,1)}) %reduce-scatter.25.cloned.1.call-update) | async-done | bytes 5136
  1803.6 14.0 all-reduce.4
  1817.8 11.2 all-reduce.6
  1833.3 277.0 %all-reduce.10.cloned.1.call-done = (bf16[160,1280]{1,0:T(8,128)(2,1)}, bf16[160,1280]{1,0:T(8,128)(2,1)}, bf16[160,1280]{1,0:T(8,128)(2,1)}, bf16[160,1280]{1,0...) async-done(((bf16[160,1280]{1,0:T(8,128)(2,1)}, ...) | async-done | bytes 16261136 | tf_op jit(solution)/shard_map/psum | solution.py:448
  2120.8 5.2 convert_element_type.363
  2126.0 4.2 convert_element_type.365
  2130.3 4.4 convert_element_type.367
  (377 shorter events, 174.0 us)
Async XLA Ops:
  7.2 45.0 %all-gather.13.cloned.1.call-start = ((), (), s32[]{:S(2)}) async-start(), calls=%async_computation.14 | async-start | bytes 3686400 | tf_op jit(solution)/shard_map/all_gather | solution.py:120
  7.9 84.3 %all-gather.11.cloned.1.call-start = ((), (), s32[]{:S(2)}) async-start(), calls=%async_computation.13 | async-start | bytes 3686400 | tf_op jit(solution)/shard_map/all_gather | solution.py:119
  8.7 202.4 %all-gather.9.cloned.1.call-start = ((), (), s32[]{:S(2)}) async-start(), calls=%async_computation.12 | async-start | bytes 3686400 | tf_op jit(solution)/shard_map/all_gather | solution.py:121
  9.4 297.4 %all-gather.15.cloned.1.call-start = ((), (), s32[]{:S(2)}) async-start(), calls=%async_computation.15 | async-start | bytes 3686400 | tf_op jit(solution)/shard_map/all_gather | solution.py:122
  10.0 42.2 %copy-start.8 = (bf16[256,1280]{1,0:T(8,128)(2,1)S(1)}, bf16[256,1280]{1,0:T(8,128)(2,1)}, u32[]{:S(2)}) copy-start(bf16[256,1280]{1,0:T(8,128)(2,1)} %param.19) | copy-start | bytes 1966084
  12.0 199.1 %copy-start.65 = (f32[256]{0:T(256)}, f32[256]{0:T(256)S(1)}, u32[]{:S(2)}) copy-start(f32[256]{0:T(256)S(1)} %get-tuple-element.69) | copy-start | bytes 3076
  34.9 176.2 %copy-start.51 = (f32[1280]{0:T(1024)}, f32[1280]{0:T(1024)S(1)}, u32[]{:S(2)}) copy-start(f32[1280]{0:T(1024)S(1)} %convert_element_type.288) | copy-start | bytes 15364
  37.0 9.7 copy-start.36
  46.8 49.1 %copy-start.29 = (f32[256,128]{0,1:T(8,128)}, f32[256,128]{0,1:T(8,128)S(1)}, u32[]{:S(2)}) copy-start(f32[256,128]{0,1:T(8,128)S(1)} %get-tuple-element.88) | copy-start | bytes 393220
  97.3 197.1 %copy-start.16 = (bf16[256,10,128]{0,2,1:T(8,128)(2,1)}, bf16[256,10,128]{0,2,1:T(8,128)(2,1)S(1)}, u32[]{:S(2)}) copy-start(bf16[256,10,128]{0,2,1:T(8,128)(2,1)S(1)} %get-tuple-element.61) | copy-start | bytes 1966084
  102.5 114.7 %copy-start.37 = (s32[256,7]{1,0:T(8,128)S(1)}, s32[256,7]{1,0:T(8,128)}, u32[]{:S(2)}) copy-start(s32[256,7]{1,0:T(8,128)} %copy-done.36) | copy-start | bytes 21508
  102.5 114.9 %collective-permute-start.7 = (bf16[256,1280]{1,0:T(8,128)(2,1)S(1)}, bf16[256,1280]{1,0:T(8,128)(2,1)S(1)}, u32[]{:S(2)}, u32[]{:S(2)}) collective-permute-start(bf16[256,1280]{1,0:T(8,128)(2,1)S(1)} %add_convert_fusion.1), channel_id=1, source_target_pairs={{0,1},{1,2},{2,3},{3,4},{4,5},{5,6},{6,7},{7,8},{8,9},{9,10},{10,1... | collective-permute-start | bytes 1966088 | tf_op jit(solution)/shard_map/ppermute | solution.py:19
  105.4 114.1 %collective-permute-start.6 = (bf16[256,1280]{1,0:T(8,128)(2,1)S(1)}, bf16[256,1280]{1,0:T(8,128)(2,1)}, u32[]{:S(2)}, u32[]{:S(2)}) collective-permute-start(bf16[256,1280]{1,0:T(8,128)(2,1)S(1)} %add_convert_fusion.1), channel_id=1, source_target_pairs={{0,2},{1,3},{2,4},{3,5},{4,6},{5,7},{6,8},{7,9},{8,10},{9,11},{10,... | collective-permute-start | bytes 1966088 | tf_op jit(solution)/shard_map/ppermute | solution.py:19
  108.5 127.1 %collective-permute-start.5 = (bf16[256,1280]{1,0:T(8,128)(2,1)S(1)}, bf16[256,1280]{1,0:T(8,128)(2,1)}, u32[]{:S(2)}, u32[]{:S(2)}) collective-permute-start(bf16[256,1280]{1,0:T(8,128)(2,1)S(1)} %add_convert_fusion.1), channel_id=1, source_target_pairs={{0,3},{1,4},{2,5},{3,6},{4,7},{5,8},{6,9},{7,10},{8,11},{9,12},{10... | collective-permute-start | bytes 1966088 | tf_op jit(solution)/shard_map/ppermute | solution.py:19
  111.4 130.8 %collective-permute-start.4 = (bf16[256,1280]{1,0:T(8,128)(2,1)S(1)}, bf16[256,1280]{1,0:T(8,128)(2,1)}, u32[]{:S(2)}, u32[]{:S(2)}) collective-permute-start(bf16[256,1280]{1,0:T(8,128)(2,1)S(1)} %add_convert_fusion.1), channel_id=1, source_target_pairs={{0,4},{1,5},{2,6},{3,7},{4,8},{5,9},{6,10},{7,11},{8,12},{9,13},{1... | collective-permute-start | bytes 1966088 | tf_op jit(solution)/shard_map/ppermute | solution.py:19
  214.9 29.7 %collective-permute-start = (bf16[256,1280]{1,0:T(8,128)(2,1)}, bf16[256,1280]{1,0:T(8,128)(2,1)}, u32[]{:S(2)}, u32[]{:S(2)}) collective-permute-start(bf16[256,1280]{1,0:T(8,128)(2,1)} %convolution_convert_fusion.9), channel_id=1, source_target_pairs={{0,4},{1,5},{2,6},{3,7},{4,8},{5,9},{6,10},{7,11},{8,12},{9,13},{1... | collective-permute-start | bytes 1966088 | tf_op jit(solution)/shard_map/ppermute | solution.py:19
  217.4 9.6 copy-start.41
  217.4 34.6 %collective-permute-start.1 = (bf16[256,1280]{1,0:T(8,128)(2,1)}, bf16[256,1280]{1,0:T(8,128)(2,1)}, u32[]{:S(2)}, u32[]{:S(2)}) collective-permute-start(bf16[256,1280]{1,0:T(8,128)(2,1)} %convolution_convert_fusion.9), channel_id=1, source_target_pairs={{0,3},{1,4},{2,5},{3,6},{4,7},{5,8},{6,9},{7,10},{8,11},{9,12},{10... | collective-permute-start | bytes 1966088 | tf_op jit(solution)/shard_map/ppermute | solution.py:19
  219.5 60.5 %collective-permute-start.2 = (bf16[256,1280]{1,0:T(8,128)(2,1)}, bf16[256,1280]{1,0:T(8,128)(2,1)}, u32[]{:S(2)}, u32[]{:S(2)}) collective-permute-start(bf16[256,1280]{1,0:T(8,128)(2,1)} %convolution_convert_fusion.9), channel_id=1, source_target_pairs={{0,2},{1,3},{2,4},{3,5},{4,6},{5,7},{6,8},{7,9},{8,10},{9,11},{10,... | collective-permute-start | bytes 1966088 | tf_op jit(solution)/shard_map/ppermute | solution.py:19
  226.7 84.0 %copy-start.55 = (f32[1280]{0:T(1024)}, f32[1280]{0:T(1024)S(1)}, u32[]{:S(2)}) copy-start(f32[1280]{0:T(1024)S(1)} %convert_element_type.297) | copy-start | bytes 15364
  227.1 356.0 %copy-start.61 = (s32[1792]{0:T(1024)}, s32[1792]{0:T(1024)S(1)}, u32[]{:S(2)}) copy-start(s32[1792]{0:T(1024)S(1)} %fusion.83) | copy-start | bytes 21508
  235.6 46.5 %collective-permute-start.3 = (bf16[256,1280]{1,0:T(8,128)(2,1)}, bf16[256,1280]{1,0:T(8,128)(2,1)}, u32[]{:S(2)}, u32[]{:S(2)}) collective-permute-start(bf16[256,1280]{1,0:T(8,128)(2,1)} %convolution_convert_fusion.9), channel_id=1, source_target_pairs={{0,1},{1,2},{2,3},{3,4},{4,5},{5,6},{6,7},{7,8},{8,9},{9,10},{10,1... | collective-permute-start | bytes 1966088 | tf_op jit(solution)/shard_map/ppermute | solution.py:19
  311.4 269.8 %copy-start.2 = (bf16[256,1280]{1,0:T(8,128)(2,1)}, bf16[256,1280]{1,0:T(8,128)(2,1)S(1)}, u32[]{:S(2)}) copy-start(bf16[256,1280]{1,0:T(8,128)(2,1)S(1)} %multiply_convert_fusion.3) | copy-start | bytes 1966084
  339.1 20.0 copy-start.72
  339.1 227.1 %copy-start.14 = (bf16[256,1280]{1,0:T(8,128)(2,1)S(1)}, bf16[256,1280]{1,0:T(8,128)(2,1)}, u32[]{:S(2)}) copy-start(bf16[256,1280]{1,0:T(8,128)(2,1)} %param.20) | copy-start | bytes 1966084
  339.1 268.4 %all-to-all-start = ((bf16[8,2,224,1280]{3,2,1,0:T(8,128)(2,1)}), bf16[8,2,224,1280]{3,2,1,0:T(8,128)(2,1)}, u32[]{:S(2)}, u32[]{:S(2)}) async-start(bf16[8,2,224,1280]{3,2,1,0:T(8,128)(2,1)} %bitcast.211), calls=%async_computation | async-start | bytes 18350080 | tf_op jit(solution)/shard_map/all_to_all | solution.py:197
  566.2 15.0 copy-start.47
  570.9 10.6 copy-start.57
  582.9 24.6 %copy-start.34 = (f32[256,7]{1,0:T(8,128)}, f32[256,7]{1,0:T(8,128)S(1)}, u32[]{:S(2)}) copy-start(f32[256,7]{1,0:T(8,128)S(1)} %copy.175) | copy-start | bytes 21508
  607.5 21.7 %slice-start.8 = ((s8[4587520]{0:T(1024)(128)(4,1)}), s8[393216]{0:T(1024)(128)(4,1)S(1)}, s32[]{:S(2)}) async-start(s8[4587520]{0:T(1024)(128)(4,1)} %bitcast.247), calls=%async_computation.36 | async-start | bytes 786432
  607.5 206.1 %all-to-all-start.2 = ((bf16[8,2,224,1280]{3,2,1,0:T(8,128)(2,1)}), bf16[8,2,224,1280]{3,2,1,0:T(8,128)(2,1)}, u32[]{:S(2)}, u32[]{:S(2)}) async-start(bf16[8,2,224,1280]{3,2,1,0:T(8,128)(2,1)} %bitcast.210), calls=%async_computation.2 | async-start | bytes 18350080 | tf_op jit(solution)/shard_map/all_to_all | solution.py:248
  612.9 16.4 slice-start.9
  860.2 261.1 %all-to-all-start.1 = ((bf16[8,2,224,1280]{3,2,1,0:T(8,128)(2,1)}), bf16[8,2,224,1280]{3,2,1,0:T(8,128)(2,1)}, u32[]{:S(2)}, u32[]{:S(2)}) async-start(bf16[8,2,224,1280]{3,2,1,0:T(8,128)(2,1)} %copy.181), calls=%async_computation.1 | async-start | bytes 18350080 | tf_op jit(solution)/shard_map/all_to_all | solution.py:207
  865.2 261.2 %all-gather.19.cloned.1.call-start = ((), (), s32[]{:S(2)}) async-start(), calls=%async_computation.17 | async-start | bytes 2580480 | tf_op jit(solution)/shard_map/all_gather | solution.py:126
  865.8 264.1 %all-gather.17.cloned.1.call-start = ((), (), s32[]{:S(2)}) async-start(), calls=%async_computation.16 | async-start | bytes 2580480 | tf_op jit(solution)/shard_map/all_gather | solution.py:125
  866.4 266.9 %all-gather.21.cloned.1.call-start = ((), (), s32[]{:S(2)}) async-start(), calls=%async_computation.18 | async-start | bytes 2580480 | tf_op jit(solution)/shard_map/all_gather | solution.py:127
  910.2 216.3 %copy-start.3 = (bf16[256,1280]{1,0:T(8,128)(2,1)S(1)}, bf16[256,1280]{1,0:T(8,128)(2,1)}, u32[]{:S(2)}) copy-start(bf16[256,1280]{1,0:T(8,128)(2,1)} %copy-done.2) | copy-start | bytes 1966084
  1121.3 248.8 %all-to-all-start.3 = ((bf16[8,2,224,1280]{3,2,1,0:T(8,128)(2,1)}), bf16[8,2,224,1280]{3,2,1,0:T(8,128)(2,1)}, u32[]{:S(2)}, u32[]{:S(2)}) async-start(bf16[8,2,224,1280]{3,2,1,0:T(8,128)(2,1)} %copy.186), calls=%async_computation.3 | async-start | bytes 18350080 | tf_op jit(solution)/shard_map/all_to_all | solution.py:292
  1126.3 531.4 %reduce-scatter.21.cloned.1.call-start = ((), (), s32[]{:S(2)}) async-start(), calls=%async_computation.24 | async-start | bytes 2580480 | tf_op jit(solution)/shard_map/reduce_scatter | solution.py:439
  1138.9 518.9 %reduce-scatter.19.cloned.1.call-start = ((), (), s32[]{:S(2)}) async-start(), calls=%async_computation.23 | async-start | bytes 2580480 | tf_op jit(solution)/shard_map/reduce_scatter | solution.py:436
  1141.2 516.6 %reduce-scatter.23.cloned.1.call-start = ((), (), s32[]{:S(2)}) async-start(), calls=%async_computation.25 | async-start | bytes 2580480 | tf_op jit(solution)/shard_map/reduce_scatter | solution.py:442
  1143.5 514.3 %reduce-scatter.17.cloned.1.call-start = ((), (), s32[]{:S(2)}) async-start(), calls=%async_computation.22 | async-start | bytes 3686400 | tf_op jit(solution)/shard_map/reduce_scatter | solution.py:427
  1407.5 250.3 %reduce-scatter.11.cloned.1.call-start = ((), (), s32[]{:S(2)}) async-start(), calls=%async_computation.19 | async-start | bytes 3686400 | tf_op jit(solution)/shard_map/reduce_scatter | solution.py:418
  1414.7 11.6 slice-start
  1414.7 11.6 slice-start.1
  1414.8 13.1 slice-start.2
  1414.8 13.1 slice-start.3
  1445.2 277.0 %reduce-scatter.15.cloned.1.call-start = ((), (), s32[]{:S(2)}) async-start(), calls=%async_computation.21 | async-start | bytes 3686400 | tf_op jit(solution)/shard_map/reduce_scatter | solution.py:424
  1451.7 49.4 %collective-permute-start.15 = (bf16[256,1280]{0,1:T(8,128)(2,1)S(1)}, bf16[256,1280]{0,1:T(8,128)(2,1)S(1)}, u32[]{:S(2)}, u32[]{:S(2)}) collective-permute-start(bf16[256,1280]{0,1:T(8,128)(2,1)S(1)} %bitcast.241), channel_id=1, source_target_pairs={{4,0},{5,1},{6,2},{7,3},{8,4},{9,5},{10,6},{11,7},{12,8},{13,9},{1... | collective-permute-start | bytes 1966088 | tf_op jit(solution)/shard_map/ppermute | solution.py:19
  1453.0 48.1 %collective-permute-start.12 = (bf16[256,1280]{0,1:T(8,128)(2,1)S(1)}, bf16[256,1280]{0,1:T(8,128)(2,1)S(1)}, u32[]{:S(2)}, u32[]{:S(2)}) collective-permute-start(bf16[256,1280]{0,1:T(8,128)(2,1)S(1)} %bitcast.239), channel_id=1, source_target_pairs={{1,0},{2,1},{3,2},{4,3},{5,4},{6,5},{7,6},{8,7},{9,8},{10,9},{11,1... | collective-permute-start | bytes 1966088 | tf_op jit(solution)/shard_map/ppermute | solution.py:19
  1454.3 51.0 %collective-permute-start.14 = (bf16[256,1280]{0,1:T(8,128)(2,1)S(1)}, bf16[256,1280]{0,1:T(8,128)(2,1)S(1)}, u32[]{:S(2)}, u32[]{:S(2)}) collective-permute-start(bf16[256,1280]{0,1:T(8,128)(2,1)S(1)} %bitcast.237), channel_id=1, source_target_pairs={{3,0},{4,1},{5,2},{6,3},{7,4},{8,5},{9,6},{10,7},{11,8},{12,9},{13... | collective-permute-start | bytes 1966088 | tf_op jit(solution)/shard_map/ppermute | solution.py:19
  1455.6 70.7 %collective-permute-start.13 = (bf16[256,1280]{0,1:T(8,128)(2,1)S(1)}, bf16[256,1280]{0,1:T(8,128)(2,1)S(1)}, u32[]{:S(2)}, u32[]{:S(2)}) collective-permute-start(bf16[256,1280]{0,1:T(8,128)(2,1)S(1)} %bitcast.235), channel_id=1, source_target_pairs={{2,0},{3,1},{4,2},{5,3},{6,4},{7,5},{8,6},{9,7},{10,8},{11,9},{12,... | collective-permute-start | bytes 1966088 | tf_op jit(solution)/shard_map/ppermute | solution.py:19
  1529.6 235.1 %reduce-scatter.13.cloned.1.call-start = ((), (), s32[]{:S(2)}) async-start(), calls=%async_computation.20 | async-start | bytes 3686400 | tf_op jit(solution)/shard_map/reduce_scatter | solution.py:421
  1534.0 61.6 %collective-permute-start.11 = (bf16[256,1280]{0,1:T(8,128)(2,1)S(1)}, bf16[256,1280]{0,1:T(8,128)(2,1)S(1)}, u32[]{:S(2)}, u32[]{:S(2)}) collective-permute-start(bf16[256,1280]{0,1:T(8,128)(2,1)S(1)} %bitcast.242), channel_id=1, source_target_pairs={{4,0},{5,1},{6,2},{7,3},{8,4},{9,5},{10,6},{11,7},{12,8},{13,9},{1... | collective-permute-start | bytes 1966088 | tf_op jit(solution)/shard_map/ppermute | solution.py:19
  1535.3 60.3 %collective-permute-start.8 = (bf16[256,1280]{0,1:T(8,128)(2,1)S(1)}, bf16[256,1280]{0,1:T(8,128)(2,1)S(1)}, u32[]{:S(2)}, u32[]{:S(2)}) collective-permute-start(bf16[256,1280]{0,1:T(8,128)(2,1)S(1)} %bitcast.240), channel_id=1, source_target_pairs={{1,0},{2,1},{3,2},{4,3},{5,4},{6,5},{7,6},{8,7},{9,8},{10,9},{11,1... | collective-permute-start | bytes 1966088 | tf_op jit(solution)/shard_map/ppermute | solution.py:19
  1536.8 58.8 %collective-permute-start.10 = (bf16[256,1280]{0,1:T(8,128)(2,1)S(1)}, bf16[256,1280]{0,1:T(8,128)(2,1)S(1)}, u32[]{:S(2)}, u32[]{:S(2)}) collective-permute-start(bf16[256,1280]{0,1:T(8,128)(2,1)S(1)} %bitcast.238), channel_id=1, source_target_pairs={{3,0},{4,1},{5,2},{6,3},{7,4},{8,5},{9,6},{10,7},{11,8},{12,9},{13... | collective-permute-start | bytes 1966088 | tf_op jit(solution)/shard_map/ppermute | solution.py:19
  1538.1 66.3 %collective-permute-start.9 = (bf16[256,1280]{0,1:T(8,128)(2,1)S(1)}, bf16[256,1280]{0,1:T(8,128)(2,1)S(1)}, u32[]{:S(2)}, u32[]{:S(2)}) collective-permute-start(bf16[256,1280]{0,1:T(8,128)(2,1)S(1)} %bitcast.236), channel_id=1, source_target_pairs={{2,0},{3,1},{4,2},{5,3},{6,4},{7,5},{8,6},{9,7},{10,8},{11,9},{12,... | collective-permute-start | bytes 1966088 | tf_op jit(solution)/shard_map/ppermute | solution.py:19
  1539.5 65.3 %copy-start.40 = (f32[256,128]{0,1:T(8,128)S(1)}, f32[256,128]{0,1:T(8,128)}, u32[]{:S(2)}) copy-start(f32[256,128]{0,1:T(8,128)} %get-tuple-element.65) | copy-start | bytes 393220
  1608.9 187.9 %reduce-scatter.25.cloned.1.call-start = ((), (), s32[]{:S(2)}) async-start(), calls=%async_computation.26 | async-start | bytes 368640
  1625.1 15.6 copy-start.4
  1641.8 468.5 %all-reduce.10.cloned.1.call-start = ((), (), s32[]{:S(2)}) async-start(), calls=%async_computation.27 | async-start | bytes 32522240 | tf_op jit(solution)/shard_map/psum | solution.py:448
  1801.2 29.6 %copy-start.13 = (f32[256,1280]{1,0:T(8,128)S(1)}, f32[256,1280]{1,0:T(8,128)}, u32[]{:S(2)}) copy-start(f32[256,1280]{1,0:T(8,128)} %copy-done.12) | copy-start | bytes 3932164
  1801.2 29.6 %copy-start.74 = (f32[256]{0:T(256)S(1)}, f32[256]{0:T(256)}, u32[]{:S(2)}) copy-start(f32[256]{0:T(256)} %get-tuple-element.68) | copy-start | bytes 3076
  2110.3 9.5 copy-start.44
  (59 other events, 269.2 us)
Sparse Core Ops, SparseCore 0:
  9.7 42.4 all-gather.12
  53.8 38.3 all-gather.10
  93.9 117.1 all-gather.8
  212.6 82.4 all-gather.14
  867.4 82.1 all-gather.18
  951.1 107.7 all-gather.16
  1060.6 41.0 all-gather.20
  1139.0 102.3 reduce-scatter.20
  1243.7 90.8 reduce-scatter.18
  1336.7 67.8 reduce-scatter.22
  1407.6 121.4 reduce-scatter.16
  1531.4 120.3 reduce-scatter.10
  1654.1 68.0 reduce-scatter.14
  1724.5 40.1 reduce-scatter.12
  1767.4 29.3 reduce-scatter.24
  1803.5 306.7 all-reduce.9
where the time goes:
time: 2150 us; the launch traced here: 2140 us
  waiting for transfers between devices  1280 us (60%)
  matrix products  253 us (12%)
  blocking collectives  251 us (12%)
  local copies, waits for them, and re-layouts  166 us (8%)
  other arithmetic  99.2 us (5%)
  starting transfers between devices  74.6 us (3%)
    psum x1, waiting for transfers between devices, per_device(): lax.psum(shares[1].astype(jnp.bfloat16), 'rep').astype(jnp.float32)  277 us
    all_to_all x1, waiting for transfers between devices, per_device(): lax.all_to_all(out_rows, 'fsdp', split_axis=0, concat_axis=0, tiled=True)  211 us
    all_gather x1, blocking collectives, per_device(): lax.all_gather(w_router, 'fsdp', axis=0, tiled=True)  207 us
    all_to_all x1, waiting for transfers between devices, per_device(): lax.all_to_all(input_rows, 'fsdp', split_axis=0, concat_axis=0, tiled=True)  190 us
    all_to_all x1, waiting for transfers between devices, per_device(): lax.all_to_all(send_grads, 'fsdp', split_axis=0, concat_axis=0, tiled=True)  169 us
    ppermute x16, waiting for transfers between devices, shifted(): return lax.ppermute(block, axis, route)  166 us
    all_gather x1, waiting for transfers between devices, per_device(): lax.all_gather(w_value, 'fsdp', axis=0, tiled=True)  94.3 us
    reduce_scatter x1, waiting for transfers between devices, per_device(): lax.psum_scatter(value_term.astype(jnp.bfloat16), 'fsdp', scatter_dimensi...  64.4 us
  transfers between devices with their start and end apart: 36, of which 17 were waited for; matrix products, arithmetic and copies ran while one was open for 19% of the time, Pallas kernels for 0%

commit v1 on v0

v1 whole, which is shorter than its diff:
```python
import math

import jax
import jax.numpy as jnp
from jax import lax
from jax.sharding import PartitionSpec as P

DH = 128
SEQ_MAX = 1024


EPSILON = 1e-06
NEGATIVE = -1e30


def shifted(block, axis, distance):
    devices = range(lax.axis_size(axis))
    route = [(i - distance, i) for i in devices if i - distance in devices]
    return lax.ppermute(block, axis, route)


def shifted_back(block, axis, distance):
    devices = range(lax.axis_size(axis))
    route = [(i, i - distance) for i in devices if i - distance in devices]
    return lax.ppermute(block, axis, route)


def rms_scale(values):
    return lax.rsqrt(jnp.mean(values * values, axis=1, keepdims=True) + EPSILON)


def silu_value(values):
    return values / (1.0 + jnp.exp(-values))


def rotary_tables(position, head_size):
    half_size = head_size // 2
    frequency = 1.0 / 10000.0 ** (jnp.arange(half_size, dtype=jnp.float32) / half_size)
    angles = position.astype(jnp.float32)[:, None] * frequency[None, :]
    cosine_table = jnp.cos(angles)
    sine_table = jnp.sin(angles)
    cosine_table = jnp.concatenate([cosine_table, cosine_table], axis=1)[:, None, :]
    sine_table = jnp.concatenate([sine_table, sine_table], axis=1)[:, None, :]
    return (cosine_table, sine_table)


def rotate(values, cosine_table, sine_table):
    half_size = values.shape[-1] // 2
    turned = jnp.concatenate([-values[..., half_size:], values[..., :half_size]], axis=-1)
    return values * cosine_table + turned * sine_table


def rotate_back(values, cosine_table, sine_table):
    half_size = values.shape[-1] // 2
    scaled = values * sine_table
    turned = jnp.concatenate([scaled[..., half_size:], -scaled[..., :half_size]], axis=-1)
    return values * cosine_table + turned


def norm_back(grad_rows, values, scale_rows, gain_vector):
    weighted = grad_rows * gain_vector[None, :]
    gain_grad = jnp.sum(grad_rows * values * scale_rows, axis=0)
    inner_mean = jnp.mean(weighted * values, axis=1, keepdims=True)
    return (
        scale_rows * weighted - values * (scale_rows * scale_rows * scale_rows) * inner_mean,
        gain_grad,
    )


def sequence_starts(lengths, sequence_order, token_index):
    seq_count = lengths.shape[0]
    picker = sequence_order[:, None] == jnp.arange(seq_count, dtype=jnp.int32)[None, :]
    ordered = jnp.sum(jnp.where(picker, lengths[None, :], 0), axis=1)
    opening = jnp.cumsum(ordered) - ordered
    chosen_open = jnp.where(opening[None, :] <= token_index[:, None], opening[None, :], 0)
    return jnp.max(chosen_open, axis=1)


def project(left, right):
    return jnp.dot(left, right, preferred_element_type=jnp.float32)


def gather(block, axis):
    return lax.all_gather(block, axis, axis=0, tiled=True)


def scatter(block, axis):
    return lax.psum_scatter(block, axis, scatter_dimension=0, tiled=True)


def per_device(
    tokens,
    cotangent,
    lengths,
    sequence_order,
    expert_choice,
    expert_home,
    first_gain,
    w_query,
    w_key,
    w_value,
    w_out,
    second_gain,
    w_router,
    shared_gate,
    shared_up,
    shared_down,
    expert_gate,
    expert_up,
    expert_down,
):
    tok_rows, width = tokens.shape
    experts = expert_home.shape[0]
    local_experts = expert_gate.shape[0]
    hidden = expert_gate.shape[2]
    groups = lax.axis_size("fsdp")
    shard = w_query.shape[0]
    slice_size = shared_down.shape[0]
    att_width = w_query.shape[1]
    heads = att_width // DH
    reach = (SEQ_MAX + tok_rows - 2) // tok_rows
    window = (reach + 1) * tok_rows
    inv_root = 1.0 / math.sqrt(DH)
    place = lax.axis_index("fsdp")
    device = lax.axis_index("rep") * groups + place
    window_parts = [tokens]
    for distance in range(1, reach + 1):
        window_parts.insert(0, shifted(tokens, ("rep", "fsdp"), distance))
    window_tokens = jnp.concatenate(window_parts, axis=0)
    qkv_full = gather(jnp.concatenate([w_query, w_key, w_value], axis=1), "fsdp")
    pad = 128 - experts - 2
    small = jnp.concatenate(
        [
            w_out,
            w_router,
            first_gain[:, None],
            second_gain[:, None],
            jnp.zeros((shard, pad), jnp.bfloat16),
        ],
        axis=1,
    )
    small_full = gather(small, "fsdp")
    out_full = small_full[:, :width]
    router_full = small_full[:, width : width + experts]
    gain_one = small_full[:, width + experts].astype(jnp.float32)
    gain_two = small_full[:, width + experts + 1].astype(jnp.float32)
    shared_pair = jnp.concatenate(
        [
            shared_gate.reshape(shard, groups, slice_size).transpose(1, 0, 2),
            shared_up.reshape(shard, groups, slice_size).transpose(1, 0, 2),
        ],
        axis=2,
    )
    shared_cut = lax.all_to_all(
        shared_pair, "fsdp", split_axis=0, concat_axis=0, tiled=True
    ).reshape(groups * shard, 2 * slice_size)
    cot_all = gather(cotangent, "fsdp")
    choice_all = gather(expert_choice, "fsdp")

    query_index = device * tok_rows + jnp.arange(tok_rows, dtype=jnp.int32)
    key_index = (device - reach) * tok_rows + jnp.arange(window, dtype=jnp.int32)
    start_key = sequence_starts(lengths, sequence_order, key_index)
    start_query = start_key[reach * tok_rows :]
    visible = (
        (key_index[None, :] <= query_index[:, None]) & (key_index[None, :] >= start_query[:, None])
    )[None, :, :]
    cosine_table, sine_table = rotary_tables(key_index - start_key, DH)
    cosine_own = cosine_table[reach * tok_rows :]
    sine_own = sine_table[reach * tok_rows :]

    window_input = window_tokens.astype(jnp.float32)
    normed_window = (window_input * rms_scale(window_input) * gain_one[None, :]).astype(
        jnp.bfloat16
    )
    layer_input = tokens.astype(jnp.float32)
    scale_one = rms_scale(layer_input)
    normed_one = (layer_input * scale_one * gain_one[None, :]).astype(jnp.bfloat16)
    query_raw = project(normed_one, qkv_full[:, :att_width]).reshape(tok_rows, heads, DH)
    key_raw = project(normed_window, qkv_full[:, att_width : 2 * att_width]).reshape(
        window, heads, DH
    )
    value_window = (
        project(normed_window, qkv_full[:, 2 * att_width :])
        .astype(jnp.bfloat16)
        .reshape(window, heads, DH)
    )
    query_rot = rotate(query_raw, cosine_own, sine_own).astype(jnp.bfloat16)
    key_window = rotate(key_raw, cosine_table, sine_table).astype(jnp.bfloat16)
    scores = (
        jnp.einsum("qhd,khd->hqk", query_rot, key_window, preferred_element_type=jnp.float32)
        * inv_root
    )
    masked = jnp.where(visible, scores, NEGATIVE)
    top_score = jnp.max(masked, axis=2, keepdims=True)
    expanded = jnp.exp(masked - top_score)
    denominator = jnp.sum(expanded, axis=2, keepdims=True)
    log_total = top_score + jnp.log(denominator)
    probs_low = (expanded / denominator).astype(jnp.bfloat16)
    mixed_rows = jnp.einsum(
        "hqk,khd->qhd", probs_low, value_window, preferred_element_type=jnp.float32
    )
    attended = mixed_rows.astype(jnp.bfloat16).reshape(tok_rows, att_width)
    resid_one = layer_input + project(attended, out_full)
    scale_two = rms_scale(resid_one)
    normed_two = (resid_one * scale_two * gain_two[None, :]).astype(jnp.bfloat16)
    normed_all = gather(normed_two, "fsdp")

    logits_all = project(normed_all, router_full)
    chosen = jnp.any(
        choice_all[:, :, None] == jnp.arange(experts, dtype=jnp.int32)[None, None, :], axis=1
    )
    gates_all = jax.nn.softmax(jnp.where(chosen, logits_all, NEGATIVE), axis=1)
    slots = place * local_experts + jnp.arange(local_experts, dtype=jnp.int32)
    slot_pick = (expert_home[:, None] == slots[None, :]).astype(jnp.float32)
    gate_slots = jnp.sum(gates_all[:, :, None] * slot_pick[None, :, :], axis=1)

    tail = -(local_experts * hidden + slice_size) % 128
    gate_weight = jnp.concatenate(
        [expert_gate[j] for j in range(local_experts)]
        + [shared_cut[:, :slice_size], jnp.zeros((width, tail), jnp.bfloat16)],
        axis=1,
    )
    up_weight = jnp.concatenate(
        [expert_up[j] for j in range(local_experts)]
        + [shared_cut[:, slice_size:], jnp.zeros((width, tail), jnp.bfloat16)],
        axis=1,
    )
    down_weight = jnp.concatenate(
        [expert_down.reshape(local_experts * hidden, width), shared_down]
        + [jnp.zeros((tail, width), jnp.bfloat16)],
        axis=0,
    )
    down_back = jnp.einsum("td,fd->tf", cot_all, down_weight, preferred_element_type=jnp.float32)
    group_rows = normed_all.shape[0]
    gate_scale = jnp.concatenate(
        [
            jnp.broadcast_to(gate_slots[:, j : j + 1], (group_rows, hidden))
            for j in range(local_experts)
        ]
        + [jnp.ones((group_rows, slice_size + tail), jnp.float32)],
        axis=1,
    )
    pre_gate = project(normed_all, gate_weight)
    pre_up = project(normed_all, up_weight)
    sigmoid = 1.0 / (1.0 + jnp.exp(-pre_gate))
    active = silu_value(pre_gate)
    hidden_rows = (active * pre_up).astype(jnp.bfloat16).astype(jnp.float32)
    gate_grad_slots = jnp.stack(
        [
            jnp.sum(
                hidden_rows[:, j * hidden : (j + 1) * hidden]
                * down_back[:, j * hidden : (j + 1) * hidden],
                axis=1,
            )
            for j in range(local_experts)
        ],
        axis=1,
    )
    hidden_scaled = (hidden_rows * gate_scale).astype(jnp.bfloat16)
    hidden_grad = down_back * gate_scale
    gate_low = (hidden_grad * pre_up * sigmoid * (1.0 + pre_gate * (1.0 - sigmoid))).astype(
        jnp.bfloat16
    )
    up_low = (hidden_grad * active).astype(jnp.bfloat16)
    input_part = jnp.einsum("tf,df->td", gate_low, gate_weight, preferred_element_type=jnp.float32)
    input_part = input_part + jnp.einsum(
        "tf,df->td", up_low, up_weight, preferred_element_type=jnp.float32
    )
    gate_grad_part = jnp.sum(gate_grad_slots[:, None, :] * slot_pick[None, :, :], axis=2)
    gate_grad_high = gate_grad_part.astype(jnp.bfloat16)
    gate_grad_rest = (gate_grad_part - gate_grad_high.astype(jnp.float32)).astype(jnp.bfloat16)
    input_sum = scatter(
        jnp.concatenate(
            [
                input_part.astype(jnp.bfloat16),
                gate_grad_high,
                gate_grad_rest,
                jnp.zeros((group_rows, -2 * experts % 128), jnp.bfloat16),
            ],
            axis=1,
        ),
        "fsdp",
    ).astype(jnp.float32)
    output_part = project(hidden_scaled, down_weight).astype(jnp.bfloat16)
    output_sum = scatter(output_part, "fsdp").astype(jnp.float32)
    output = (resid_one + output_sum).astype(jnp.bfloat16)

    def expert_term(left, right):
        return jnp.einsum("ta,tb->ab", left, right, preferred_element_type=jnp.float32).astype(
            jnp.bfloat16
        )

    down_term = expert_term(hidden_scaled, cot_all)
    expert_down_term = down_term[: local_experts * hidden].reshape(local_experts, hidden, width)
    sdown_term = down_term[local_experts * hidden : local_experts * hidden + slice_size]
    expert_gate_term = jnp.stack(
        [
            expert_term(normed_all, gate_low[:, j * hidden : (j + 1) * hidden])
            for j in range(local_experts)
        ]
    )
    expert_up_term = jnp.stack(
        [
            expert_term(normed_all, up_low[:, j * hidden : (j + 1) * hidden])
            for j in range(local_experts)
        ]
    )
    first_cut = local_experts * hidden
    shared_terms = jnp.concatenate(
        [
            expert_term(normed_all, gate_low[:, first_cut : first_cut + slice_size]),
            expert_term(normed_all, up_low[:, first_cut : first_cut + slice_size]),
        ],
        axis=1,
    )
    shared_back = lax.all_to_all(
        shared_terms.reshape(groups, shard, 2 * slice_size),
        "fsdp",
        split_axis=0,
        concat_axis=0,
        tiled=True,
    )
    sgate_term = shared_back[:, :, :slice_size].transpose(1, 0, 2).reshape(shard, -1)
    sup_term = shared_back[:, :, slice_size:].transpose(1, 0, 2).reshape(shard, -1)

    cotan = cotangent.astype(jnp.float32)
    gates = lax.dynamic_slice_in_dim(gates_all, place * tok_rows, tok_rows, 0)
    gate_grad = (
        input_sum[:, width : width + experts]
        + input_sum[:, width + experts : width + 2 * experts]
    )
    gate_mean = jnp.sum(gates * gate_grad, axis=1, keepdims=True)
    logit_grad = (gates * (gate_grad - gate_mean)).astype(jnp.bfloat16)
    router_term = jnp.einsum(
        "td,te->de", normed_two, logit_grad, preferred_element_type=jnp.float32
    )
    normed_two_grad = input_sum[:, :width] + jnp.einsum(
        "te,de->td", logit_grad, router_full, preferred_element_type=jnp.float32
    )
    resid_part, gain_two_term = norm_back(normed_two_grad, resid_one, scale_two, gain_two)
    resid_grad = cotan + resid_part
    out_grad_low = resid_grad.astype(jnp.bfloat16)
    out_term = jnp.einsum("ta,td->ad", attended, out_grad_low, preferred_element_type=jnp.float32)
    attended_grad = (
        jnp.einsum("td,ad->ta", out_grad_low, out_full, preferred_element_type=jnp.float32)
        .astype(jnp.bfloat16)
        .reshape(tok_rows, heads, DH)
    )
    scores_back = (
        jnp.einsum("qhd,khd->hqk", query_rot, key_window, preferred_element_type=jnp.float32)
        * inv_root
    )
    probs_back = jnp.exp(jnp.where(visible, scores_back, NEGATIVE) - log_total)
    probs_back_low = probs_back.astype(jnp.bfloat16)
    probs_grad = jnp.einsum(
        "qhd,khd->hqk", attended_grad, value_window, preferred_element_type=jnp.float32
    )
    inner_sum = jnp.sum(probs_back * probs_grad, axis=2, keepdims=True)
    scores_grad = (probs_back * (probs_grad - inner_sum)).astype(jnp.bfloat16)
    query_grad_rot = (
        jnp.einsum("hqk,khd->qhd", scores_grad, key_window, preferred_element_type=jnp.float32)
        * inv_root
    )
    key_grad_rot = (
        jnp.einsum("hqk,qhd->khd", scores_grad, query_rot, preferred_element_type=jnp.float32)
        * inv_root
    )
    value_grad = (
        jnp.einsum("hqk,qhd->khd", probs_back_low, attended_grad, preferred_element_type=jnp.float32)
        .astype(jnp.bfloat16)
        .reshape(window, att_width)
    )
    query_grad = (
        rotate_back(query_grad_rot, cosine_own, sine_own)
        .astype(jnp.bfloat16)
        .reshape(tok_rows, att_width)
    )
    key_grad = (
        rotate_back(key_grad_rot, cosine_table, sine_table)
        .astype(jnp.bfloat16)
        .reshape(window, att_width)
    )
    key_value_back = jnp.einsum(
        "ta,da->td",
        jnp.concatenate([key_grad, value_grad], axis=1),
        qkv_full[:, att_width:],
        preferred_element_type=jnp.float32,
    )
    normed_one_grad = key_value_back[reach * tok_rows :] + jnp.einsum(
        "ta,da->td", query_grad, qkv_full[:, :att_width], preferred_element_type=jnp.float32
    )
    for distance in range(1, reach + 1):
        lower = (reach - distance) * tok_rows
        normed_one_grad = normed_one_grad + shifted_back(
            key_value_back[lower : lower + tok_rows].astype(jnp.bfloat16),
            ("rep", "fsdp"),
            distance,
        ).astype(jnp.float32)
    query_term = jnp.einsum("td,ta->da", normed_one, query_grad, preferred_element_type=jnp.float32)
    key_term = jnp.einsum(
        "td,ta->da", normed_window, key_grad, preferred_element_type=jnp.float32
    )
    value_term = jnp.einsum(
        "td,ta->da", normed_window, value_grad, preferred_element_type=jnp.float32
    )
    input_back, gain_one_term = norm_back(normed_one_grad, layer_input, scale_one, gain_one)
    input_grad = (resid_grad + input_back).astype(jnp.bfloat16)
    dense_share = scatter(
        jnp.concatenate(
            [
                out_term.astype(jnp.bfloat16),
                query_term.astype(jnp.bfloat16),
                key_term.astype(jnp.bfloat16),
                value_term.astype(jnp.bfloat16),
            ],
            axis=1,
        ),
        "fsdp",
    )
    small_share = scatter(
        jnp.concatenate(
            [
                router_term.astype(jnp.bfloat16),
                gain_one_term.astype(jnp.bfloat16)[:, None],
                gain_two_term.astype(jnp.bfloat16)[:, None],
                jnp.zeros((width, pad), jnp.bfloat16),
            ],
            axis=1,
        ),
        "fsdp",
    )
    summed = lax.psum(
        (
            expert_gate_term,
            expert_up_term,
            expert_down_term,
            sgate_term,
            sup_term,
            sdown_term,
            dense_share,
            small_share,
        ),
        "rep",
    )
    (
        expert_gate_sum,
        expert_up_sum,
        expert_down_sum,
        sgate_sum,
        sup_sum,
        sdown_sum,
        dense_sum,
        small_sum,
    ) = [value.astype(jnp.float32) for value in summed]
    return (
        output,
        input_grad,
        small_sum[:, experts],
        dense_sum[:, width : width + att_width],
        dense_sum[:, width + att_width : width + 2 * att_width],
        dense_sum[:, width + 2 * att_width :],
        dense_sum[:, :width],
        small_sum[:, experts + 1],
        small_sum[:, :experts],
        sgate_sum,
        sup_sum,
        sdown_sum,
        expert_gate_sum,
        expert_up_sum,
        expert_down_sum,
    )


def solution(mesh):
    placed = (
        P(("rep", "fsdp"), None),
        P(("rep", "fsdp"), None),
        P(),
        P(),
        P(("rep", "fsdp"), None),
        P(),
        P("fsdp"),
        P("fsdp", None),
        P("fsdp", None),
        P("fsdp", None),
        P("fsdp", None),
        P("fsdp"),
        P("fsdp", None),
        P("fsdp", None),
        P("fsdp", None),
        P("fsdp", None),
        P("fsdp", None, None),
        P("fsdp", None, None),
        P("fsdp", None, None),
    )
    return jax.shard_map(
        per_device,
        mesh=mesh,
        in_specs=placed,
        out_specs=(
            P(("rep", "fsdp"), None),
            P(("rep", "fsdp"), None),
            P("fsdp"),
            P("fsdp", None),
            P("fsdp", None),
            P("fsdp", None),
            P("fsdp", None),
            P("fsdp"),
            P("fsdp", None),
            P("fsdp", None),
            P("fsdp", None),
            P("fsdp", None),
            P("fsdp", None, None),
            P("fsdp", None, None),
            P("fsdp", None, None),
        ),
        check_vma=False,
    )
```

time: 2150 us -> 1310 us (0.61)
  waiting for transfers between devices: 1280 us -> 690 us
  blocking collectives: 251 us -> 52.8 us
  local copies, waits for them, and re-layouts: 166 us -> 101 us
  starting transfers between devices: 74.6 us -> 29 us
  other arithmetic: 99.2 us -> 134 us
  matrix products: 253 us -> 277 us
    all_to_all x4 -> x2, waiting for transfers between devices: 570 us -> 0.01 us  [the longest x1 0.01 us: per_device(): lax.all_to_all(shared_pair, 'fsdp', split_axis=0, concat_axis=0, tiled=True)]
    all_gather x1, blocking collectives: 207 us -> 35.1 us  [gather(): return lax.all_gather(block, axis, axis=0, tiled=True)]
    ppermute x16 -> x4, waiting for transfers between devices: 166 us -> 47.7 us  [shifted(): return lax.ppermute(block, axis, route)]
    ppermute x0 -> x4, waiting for transfers between devices: none -> 109 us  [shifted_back(): return lax.ppermute(block, axis, route)]
    dot_general x8, matrix products: 23.5 us -> 86 us  [project(): return jnp.dot(left, right, preferred_element_type=jnp.float32)]
    concatenate x1 -> x6, other arithmetic: 0.13 us -> 43.4 us  [the longest x1 31.6 us: per_device(): jnp.concatenate([out_term.astype(jnp.bfloat16), query_term.astype(jnp.bfl...]
    convert_element_type x6 -> x3, local copies, waits for them, and re-layouts: 34.3 us -> 0.25 us  [the longest x1 0.24 us: per_device(): attended_grad = jnp.einsum('td,ad->ta', out_grad_low, out_full, preferred...]
    unnamed x2 -> x0, blocking collectives: 33.1 us -> none
  transfers between devices with their start and end apart: 36 -> 19, of which waited for: 17 -> 12; matrix products, arithmetic and copies ran while one was open for 19% -> 19% of each run, Pallas kernels for 0% -> 0%
where the time goes in v1:
time: 1310 us; the launch traced here: 1300 us
  waiting for transfers between devices  690 us (53%)
  matrix products  277 us (21%)
  other arithmetic  134 us (10%)
  local copies, waits for them, and re-layouts  101 us (8%)
  blocking collectives  52.8 us (4%)
  starting transfers between devices  29 us (2%)
  between operations  15.4 us (1%)
    psum x1, waiting for transfers between devices, per_device(): lax.psum((expert_gate_term, expert_up_term, expert_down_term, sgate_term,...  306 us
    all_gather x4, waiting for transfers between devices, gather(): return lax.all_gather(block, axis, axis=0, tiled=True)  118 us
    ppermute x4, waiting for transfers between devices, shifted_back(): return lax.ppermute(block, axis, route)  109 us
    reduce_scatter x2, waiting for transfers between devices, scatter(): return lax.psum_scatter(block, axis, scatter_dimension=0, tiled=True)  97.6 us
    dot_general x8, matrix products, project(): return jnp.dot(left, right, preferred_element_type=jnp.float32)  86 us
    dot_general x7, matrix products, expert_term(): jnp.einsum('ta,tb->ab', left, right, preferred_element_type=jnp.float32)  69.7 us
    unnamed x185, local copies, waits for them, and re-layouts  49.7 us
    ppermute x4, waiting for transfers between devices, shifted(): return lax.ppermute(block, axis, route)  47.7 us
  transfers between devices with their start and end apart: 19, of which 12 were waited for; matrix products, arithmetic and copies ran while one was open for 19% of the time, Pallas kernels for 0%

profile of v1, /device:TPU:0, one launch (start us, length us, event | category | flops | bytes accessed | tf_op | source)
XLA Modules:
  0.0 1299.7 jit_solution(4447926942088302784)
XLA Ops:
  14.0 6.8 collective-permute-start
  20.8 3.5 collective-permute-start.1
  24.3 3.0 collective-permute-start.2
  27.3 2.8 collective-permute-start.3
  36.2 11.4 collective-permute-done
  48.7 18.6 %collective-permute-done.1 = bf16[256,1280]{1,0:T(8,128)(2,1)} collective-permute-done((bf16[256,1280]{1,0:T(8,128)(2,1)S(1)}, bf16[256,1280]{1,0:T(8,128)(2,1)}, u32[]{:S(2)}, u32[]{:S(2)}) %collective-permute-start.1) | collective-permute-done | bytes 655392 | tf_op jit(solution)/shard_map/ppermute | solution.py:19
  68.4 17.7 %collective-permute-done.2 = bf16[256,1280]{1,0:T(8,128)(2,1)} collective-permute-done((bf16[256,1280]{1,0:T(8,128)(2,1)S(1)}, bf16[256,1280]{1,0:T(8,128)(2,1)}, u32[]{:S(2)}, u32[]{:S(2)}) %collective-permute-start.2) | collective-permute-done | bytes 655392 | tf_op jit(solution)/shard_map/ppermute | solution.py:19
  90.9 25.8 %all-gather.5.cloned.1.call-done = bf16[1280,1408]{1,0:T(8,128)(2,1)} async-done(((bf16[160,1408]{1,0:T(8,128)(2,1)}), bf16[1280,1408]{1,0:T(8,128)(2,1)}) %all-gather.5.cloned.1.call-update) | async-done | bytes 3604496 | tf_op jit(solution)/shard_map/all_gather | solution.py:84
  118.3 91.9 %all-gather.7.cloned.1.call-done = bf16[1280,3840]{1,0:T(8,128)(2,1)} async-done(((bf16[160,3840]{1,0:T(8,128)(2,1)}), bf16[1280,3840]{1,0:T(8,128)(2,1)}) %all-gather.7.cloned.1.call-update) | async-done | bytes 9830416 | tf_op jit(solution)/shard_map/all_gather | solution.py:84
  210.2 3.7 fusion.68
  214.3 7.3 fusion.47
  224.0 2.8 fusion.125
  228.8 10.2 convolution_convert_fusion.2
  239.1 13.1 %fusion.80 = bf16[10,128,256]{2,1,0:T(8,128)(2,1)S(1)} fusion(bf16[1280,10,128]{0,2,1:T(8,128)(2,1)S(1)} %bitcast.111, f32[10,256,1280]{2,1,0:T(8,128)S(1)} %get-tuple-element.172, f32[10,256]{1,0:T(8,128)S(1)} %fusion.4, f32[10,256]{1,0:T(8,128)S(1)} %get-tuple-element.171), kind=kOutput, calls=%fused_computation.106 | convolution fusion | flops 849018880 | bytes 17059840 | tf_op jit(solution)/shard_map/hqk,khd->qhd/dot_general | solution.py:199
  257.8 3.5 all-to-all-start
  261.5 35.1 %all_gather.18 = s32[2048,7]{0,1:T(8,128)S(1)} all-gather(s32[256,7]{0,1:T(8,128)S(1)} %copy-done.63), channel_id=1, replica_groups=mesh['rep'=4,'fsdp'=8] {'fsdp'}, dimensions={0}, use_global_device_ids=true | all-gather | bytes 64512 | tf_op jit(solution)/shard_map/all_gather | solution.py:84
  296.7 4.1 slice_bitcast_fusion.2
  301.6 5.1 slice_bitcast_fusion
  307.7 7.5 concatenate.65
  315.1 8.2 concatenate.66
  323.3 16.9 %convolution_bitcast_fusion = f32[2048,1920]{0,1:T(8,128)} fusion(bf16[2048,1280]{1,0:T(8,128)(2,1)} %all-gather.11.cloned.1.call-done, bf16[112,1280]{1,0:T(8,128)(2,1)S(1)} %copy-done.69, bf16[1792,1280]{1,0:T(8,128)(2,1)} %bitcast.127, bf16[1920]{0:T(1024)(128)(2,1)S(1)} %pad.28.clone), kind=kOutput, calls=%fused_computation.19 | convolution fusion | flops 10081075200 | bytes 25849600 | tf_op jit(solution)/shard_map/td,fd->tf/dot_general | solution.py:233
  340.3 3.5 fusion.126
  344.4 15.7 %fusion.128 = f32[2048,1920]{0,1:T(8,128)} fusion(bf16[2048,1280]{0,1:T(8,128)(2,1)S(1)} %copy-done.16, bf16[1280,1920]{1,0:T(8,128)(2,1)} %concatenate.65), kind=kOutput, calls=%fused_computation.210 | convolution fusion | flops 10066329600 | bytes 25886720 | tf_op jit(solution)/shard_map/dot_general | solution.py:80
  360.1 22.0 %fusion.6 = (f32[2048,1920]{0,1:T(8,128)}, f32[2048,1920]{0,1:T(8,128)}) fusion(f32[2048,1920]{0,1:T(8,128)} %fusion.128, bf16[2048,1280]{0,1:T(8,128)(2,1)S(1)} %copy-done.16, bf16[1280,1920]{1,0:T(8,128)(2,1)S(1)} %bitcast.106), kind=kOutput, calls=%fused_computation.22 | convolution fusion | flops 10089922560 | bytes 57344000 | tf_op jit(solution)/shard_map/dot_general | solution.py:80
  382.1 10.3 fusion.8
  393.5 4.4 broadcast_in_dim.76
  397.9 25.5 %multiply_convert_fusion = (bf16[2048,1920]{0,1:T(8,128)(2,1)}, bf16[2048,1920]{0,1:T(8,128)(2,1)}) fusion(f32[2048,1920]{0,1:T(8,128)} %convolution_bitcast_fusion, f32[2048,896]{0,1:T(8,128)} %broadcast_in_dim.76, f32[2048,896]{0,1:T(8,128)S(1)} %broadcast_in_dim.74, f32[1920]{0:T(1024)S(1)} %pad.31.clone, f32[2048,1920]{0,1:T(8,128)} %fusion.128, ...), kind=kLoop, calls=%fused_computation.4 | loop fusion | flops 62914560 | bytes 77602304 | tf_op jit(solution)/shard_map/convert_element_type | solution.py:264
  423.4 17.7 %fusion.129 = f32[2048,1280]{0,1:T(8,128)} fusion(bf16[1280,1920]{1,0:T(8,128)(2,1)} %concatenate.65, bf16[2048,1920]{0,1:T(8,128)(2,1)} %get-tuple-element.130), kind=kOutput, calls=%fused_computation.211 | convolution fusion | flops 10066329600 | bytes 23265280 | tf_op jit(solution)/shard_map/tf,df->td/dot_general | solution.py:265
  441.1 14.7 %add_convert_fusion = bf16[2048,1280]{0,1:T(8,128)(2,1)S(1)} fusion(f32[2048,1280]{0,1:T(8,128)} %fusion.129, bf16[1280,1920]{1,0:T(8,128)(2,1)} %concatenate.66, bf16[2048,1920]{0,1:T(8,128)(2,1)S(1)} %copy-done.12), kind=kOutput, calls=%fused_computation.17 | convolution fusion | flops 10071572480 | bytes 28508160 | tf_op jit(solution)/shard_map/tf,df->td/dot_general | solution.py:266
  455.8 8.2 maximum_maximum_fusion.1
  464.1 22.2 %convolution_convert_fusion.5 = bf16[2048,1280]{0,1:T(8,128)(2,1)} fusion(bf16[112,1280]{1,0:T(8,128)(2,1)S(1)} %copy-done.69, bf16[1792,1280]{1,0:T(8,128)(2,1)} %bitcast.128, bf16[1920]{0:T(1024)(128)(2,1)S(1)} %pad.28.clone, f32[2048,1920]{0,1:T(8,128)} %get-tuple-element.177, f32[2048,896]{0,1:T(8,128)} %broadcast_in_dim.76, f32[2048,896]{0,1:T(8,128)} %copy-done.3, ...), kind=kOutput, calls=%fused_computation.28 | convolution fusion | flops 10099425280 | bytes 40537344 | tf_op jit(solution)/shard_map/dot_general | solution.py:80
  487.7 41.7 %reduce-scatter.11.cloned.1.call-done = bf16[256,1408]{0,1:T(8,128)(2,1)} async-done(((bf16[2048,1408]{0,1:T(8,128)(2,1)}), bf16[256,1408]{0,1:T(8,128)(2,1)}) %reduce-scatter.11.cloned.1.call-update) | async-done | bytes 720912 | tf_op jit(solution)/shard_map/reduce_scatter | solution.py:88
  533.9 55.9 %reduce-scatter.9.cloned.1.call-done = bf16[256,1280]{0,1:T(8,128)(2,1)} async-done(((bf16[2048,1280]{0,1:T(8,128)(2,1)}), bf16[256,1280]{0,1:T(8,128)(2,1)}) %reduce-scatter.9.cloned.1.call-update) | async-done | bytes 655376 | tf_op jit(solution)/shard_map/reduce_scatter | solution.py:88
  592.2 2.8 convolution_convert_fusion.4
  597.3 12.2 multiply_reduce_fusion
  611.1 3.7 fusion.24
  614.9 6.6 multiply_convert_fusion.3
  625.9 4.9 convolution_convert_fusion.1
  635.3 4.9 convolution_convert_fusion
  640.2 31.6 %pad_maximum_fusion = bf16[1280,5120]{0,1:T(8,128)(2,1)} fusion(bf16[1280,1280]{0,1:T(8,128)(2,1)S(1)} %convolution_convert_fusion, bf16[1280,1280]{0,1:T(8,128)(2,1)S(1)} %convolution_convert_fusion.1, bf16[1280,1280]{0,1:T(8,128)(2,1)S(1)} %convolution_convert_fusion.3, bf16[1280,1280]{0,1:T(8,128)(2,1)S(1)} %copy-done.4), kind=kLoop, calls=%fused_computation.9 | loop fusion | flops 52428800 | bytes 26214400 | tf_op jit(solution)/shard_map/concatenate | solution.py:409
  671.8 17.6 %copy.193 = bf16[1280,5120]{1,0:T(8,128)(2,1)} copy(bf16[1280,5120]{0,1:T(8,128)(2,1)} %pad_maximum_fusion) | data formatting | bytes 26214400
  689.6 26.9 %convolution_convert_fusion.6 = bf16[1920,1280]{1,0:T(8,128)(2,1)} fusion(bf16[2048,1280]{1,0:T(8,128)(2,1)} %all-gather.11.cloned.1.call-done, f32[2048,1920]{0,1:T(8,128)} %get-tuple-element.177, f32[2048,896]{0,1:T(8,128)} %broadcast_in_dim.76, f32[2048,896]{0,1:T(8,128)} %copy-done.3, f32[1920]{0:T(1024)S(1)} %pad.31.clone), kind=kOutput, calls=%fused_computation.29 | convolution fusion | flops 10084515840 | bytes 40574464 | tf_op jit(solution)/shard_map/ta,tb->ab/dot_general | solution.py:289
  716.5 4.8 slice.284
  723.0 4.4 convolution_convert_fusion.7
  727.4 4.4 convolution_convert_fusion.8
  732.9 3.5 all-to-all-start.1
  736.6 10.1 fusion.50
  746.7 9.9 fusion.53
  756.6 6.9 fusion.56
  763.5 14.0 %fusion.127 = (bf16[1280,1280]{0,1:T(8,128)(2,1)}, f32[1280,1280]{0,1:T(8,128)}) fusion(bf16[1280,1280]{0,1:T(8,128)(2,1)S(1)} %bitcast.110, bf16[1280,1280]{0,1:T(8,128)(2,1)} %bitcast.114, bf16[1280,3840]{1,0:T(8,128)(2,1)} %all-gather.7.cloned.1.call-done), kind=kOutput, calls=%fused_computation.209 | convolution fusion | flops 8403353600 | bytes 22937600 | tf_op jit(solution)/shard_map/ta,da->td/dot_general | solution.py:383
  784.8 7.1 fusion.59
  792.0 2.6 pad_maximum_fusion.2
  795.7 45.8 %collective-permute-done.5 = bf16[256,1280]{0,1:T(8,128)(2,1)S(1)} collective-permute-done((bf16[256,1280]{0,1:T(8,128)(2,1)S(1)}, bf16[256,1280]{0,1:T(8,128)(2,1)S(1)}, u32[]{:S(2)}, u32[]{:S(2)}) %collective-permute-start.5) | collective-permute-done | bytes 655392 | tf_op jit(solution)/shard_map/ppermute | solution.py:25
  842.9 61.6 %collective-permute-done.7 = bf16[256,1280]{0,1:T(8,128)(2,1)S(1)} collective-permute-done((bf16[256,1280]{0,1:T(8,128)(2,1)S(1)}, bf16[256,1280]{0,1:T(8,128)(2,1)S(1)}, u32[]{:S(2)}, u32[]{:S(2)}) %collective-permute-start.7) | collective-permute-done | bytes 655392 | tf_op jit(solution)/shard_map/ppermute | solution.py:25
  904.5 4.9 fusion.90
  910.4 4.9 pad_maximum_fusion.1
  917.7 4.0 copy.194
  926.6 12.4 reduce-scatter.13.cloned.1.call-done
  939.9 17.7 %psum.56 = bf16[160,128]{0,1:T(8,128)(2,1)S(1)} all-reduce(bf16[160,128]{0,1:T(8,128)(2,1)S(1)} %copy.192), channel_id=1, replica_groups=mesh['rep'=4,'fsdp'=8] {'rep'}, use_global_device_ids=true, to_apply=%region_24.25 | all-reduce | flops 20480 | bytes 81920 | tf_op jit(solution)/shard_map/psum | solution.py:432
  958.8 306.2 %all-reduce.3.cloned.1.call-done = (bf16[160,5120]{0,1:T(8,128)(2,1)}, bf16[160,896]{1,0:T(8,128)(2,1)}, bf16[160,896]{1,0:T(8,128)(2,1)}, bf16[112,1280]{1,0:T(...) async-done(((bf16[160,5120]{0,1:T(8,128)(2,1)}, bf16[160,896]{1,0:T(8,128)(2,1)}, ...) | async-done | bytes 16261136 | tf_op jit(solution)/shard_map/psum | solution.py:432
  1264.9 7.2 convert_element_type.305
  1272.1 4.2 convert_element_type.308
  1276.3 4.4 convert_element_type.309
  1282.6 2.7 copy.177
  (311 shorter events, 88.8 us)
Async XLA Ops:
  7.2 6.8 copy-start.28
  7.2 23.0 %copy-start.70 = (s32[16]{0:T(128)S(1)}, s32[16]{0:T(128)}, u32[]{:S(2)}) copy-start(s32[16]{0:T(128)} %param.21) | copy-start | bytes 196
  7.2 23.0 %copy-start.71 = (s32[16]{0:T(128)S(1)}, s32[16]{0:T(128)}, u32[]{:S(2)}) copy-start(s32[16]{0:T(128)} %param.22) | copy-start | bytes 196
  7.2 109.5 %all-gather.5.cloned.1.call-start = ((), (), s32[]{:S(2)}) async-start(), calls=%async_computation.6 | async-start | bytes 4055040 | tf_op jit(solution)/shard_map/all_gather | solution.py:84
  11.5 198.7 %all-gather.7.cloned.1.call-start = ((), (), s32[]{:S(2)}) async-start(), calls=%async_computation.7 | async-start | bytes 11059200 | tf_op jit(solution)/shard_map/all_gather | solution.py:84
  14.0 309.4 %all-gather.11.cloned.1.call-start = ((), (), s32[]{:S(2)}) async-start(), calls=%async_computation.10 | async-start | bytes 5898240 | tf_op jit(solution)/shard_map/all_gather | solution.py:84
  14.0 33.6 %collective-permute-start = (bf16[256,1280]{1,0:T(8,128)(2,1)S(1)}, bf16[256,1280]{1,0:T(8,128)(2,1)}, u32[]{:S(2)}, u32[]{:S(2)}) collective-permute-start(bf16[256,1280]{1,0:T(8,128)(2,1)S(1)} %copy-done.28), channel_id=1, source_target_pairs={{0,4},{1,5},{2,6},{3,7},{4,8},{5,9},{6,10},{7,11},{8,12},{9,13},{1... | collective-permute-start | bytes 1966088 | tf_op jit(solution)/shard_map/ppermute | solution.py:19
  20.8 46.5 %collective-permute-start.1 = (bf16[256,1280]{1,0:T(8,128)(2,1)S(1)}, bf16[256,1280]{1,0:T(8,128)(2,1)}, u32[]{:S(2)}, u32[]{:S(2)}) collective-permute-start(bf16[256,1280]{1,0:T(8,128)(2,1)S(1)} %copy-done.28), channel_id=1, source_target_pairs={{0,3},{1,4},{2,5},{3,6},{4,7},{5,8},{6,9},{7,10},{8,11},{9,12},{10... | collective-permute-start | bytes 1966088 | tf_op jit(solution)/shard_map/ppermute | solution.py:19
  24.3 61.9 %collective-permute-start.2 = (bf16[256,1280]{1,0:T(8,128)(2,1)S(1)}, bf16[256,1280]{1,0:T(8,128)(2,1)}, u32[]{:S(2)}, u32[]{:S(2)}) collective-permute-start(bf16[256,1280]{1,0:T(8,128)(2,1)S(1)} %copy-done.28), channel_id=1, source_target_pairs={{0,2},{1,3},{2,4},{3,5},{4,6},{5,7},{6,8},{7,9},{8,10},{9,11},{10,... | collective-permute-start | bytes 1966088 | tf_op jit(solution)/shard_map/ppermute | solution.py:19
  27.3 60.0 %collective-permute-start.3 = (bf16[256,1280]{1,0:T(8,128)(2,1)S(1)}, bf16[256,1280]{1,0:T(8,128)(2,1)}, u32[]{:S(2)}, u32[]{:S(2)}) collective-permute-start(bf16[256,1280]{1,0:T(8,128)(2,1)S(1)} %copy-done.28), channel_id=1, source_target_pairs={{0,1},{1,2},{2,3},{3,4},{4,5},{5,6},{6,7},{7,8},{8,9},{9,10},{10,1... | collective-permute-start | bytes 1966088 | tf_op jit(solution)/shard_map/ppermute | solution.py:19
  30.1 310.2 %all-gather.9.cloned.1.call-start = ((), (), s32[]{:S(2)}) async-start(), calls=%async_computation.8 | async-start | bytes 5898240 | tf_op jit(solution)/shard_map/all_gather | solution.py:84
  34.6 217.6 %copy-start.5 = (bf16[256,1280]{0,1:T(8,128)(2,1)}, bf16[256,1280]{0,1:T(8,128)(2,1)S(1)}, u32[]{:S(2)}) copy-start(bf16[256,1280]{0,1:T(8,128)(2,1)S(1)} %copy.152) | copy-start | bytes 1966084
  35.4 174.8 %copy-start.59 = (f32[256]{0:T(256)}, f32[256]{0:T(256)S(1)}, u32[]{:S(2)}) copy-start(f32[256]{0:T(256)S(1)} %get-tuple-element.168) | copy-start | bytes 3076
  90.9 137.9 %copy-start.64 = (f32[1280]{0:T(1024)}, f32[1280]{0:T(1024)S(1)}, u32[]{:S(2)}) copy-start(f32[1280]{0:T(1024)S(1)} %add_rsqrt_fusion) | copy-start | bytes 15364
  118.3 110.6 %copy-start.47 = (f32[1280]{0:T(1024)}, f32[1280]{0:T(1024)S(1)}, u32[]{:S(2)}) copy-start(f32[1280]{0:T(1024)S(1)} %get-tuple-element.108) | copy-start | bytes 15364
  118.3 136.0 %copy-start.51 = (f32[1280]{0:T(1024)}, f32[1280]{0:T(1024)S(1)}, u32[]{:S(2)}) copy-start(f32[1280]{0:T(1024)S(1)} %get-tuple-element.107) | copy-start | bytes 15364
  214.3 9.6 copy-start.13
  226.8 12.2 copy-start
  226.8 12.2 copy-start.49
  228.8 10.2 copy-start.53
  239.0 13.2 %copy-start.23 = (bf16[1280,1280]{0,1:T(8,128)(2,1)}, bf16[1280,1280]{0,1:T(8,128)(2,1)S(1)}, u32[]{:S(2)}) copy-start(bf16[1280,1280]{0,1:T(8,128)(2,1)S(1)} %convolution_convert_fusion.2) | copy-start | bytes 9830404
  239.1 13.2 %copy-start.40 = (bf16[1280,1408]{1,0:T(8,128)(2,1)S(1)}, bf16[1280,1408]{1,0:T(8,128)(2,1)}, u32[]{:S(2)}) copy-start(bf16[1280,1408]{1,0:T(8,128)(2,1)} %all-gather.5.cloned.1.call-done) | copy-start | bytes 10813444
  253.7 7.8 copy-start.63
  257.8 48.9 %all-to-all-start = ((bf16[8,160,224]{2,1,0:T(8,128)(2,1)}), bf16[8,160,224]{2,1,0:T(8,128)(2,1)S(1)}, u32[]{:S(2)}, u32[]{:S(2)}) async-start(bf16[8,160,224]{2,1,0:T(8,128)(2,1)} %pad_maximum_fusion.6), calls=%async_computation | async-start | bytes 1310720 | tf_op jit(solution)/shard_map/all_to_all | solution.py:154
  261.4 40.2 %copy-start.68 = (s32[16]{0:T(128)S(1)}, s32[16]{0:T(128)}, u32[]{:S(2)}) copy-start(s32[16]{0:T(128)} %param.24) | copy-start | bytes 196
  261.4 267.9 %reduce-scatter.11.cloned.1.call-start = ((), (), s32[]{:S(2)}) async-start(), calls=%async_computation.11 | async-start | bytes 6488064 | tf_op jit(solution)/shard_map/reduce_scatter | solution.py:88
  315.1 8.2 copy-start.69
  340.3 19.8 %slice-start.8 = ((s8[4915200]{0:T(1024)(128)(4,1)}), s8[4194304]{0:T(1024)(128)(4,1)S(1)}, s32[]{:S(2)}) async-start(s8[4915200]{0:T(1024)(128)(4,1)} %bitcast.105), calls=%async_computation.23 | async-start | bytes 8388608
  344.4 186.2 %copy-start.36 = (f32[2048,16]{0,1:T(8,128)}, f32[2048,16]{0,1:T(8,128)S(1)}, u32[]{:S(2)}) copy-start(f32[2048,16]{0,1:T(8,128)S(1)} %fusion.105) | copy-start | bytes 393220
  344.4 15.7 %slice-start.9 = ((s8[4915200]{0:T(1024)(128)(4,1)}), s8[720896]{0:T(1024)(128)(4,1)S(1)}, s32[]{:S(2)}) async-start(s8[4915200]{0:T(1024)(128)(4,1)} %bitcast.105), calls=%async_computation.24 | async-start | bytes 1441792
  393.5 29.9 %copy-start.3 = (f32[2048,896]{0,1:T(8,128)}, f32[2048,896]{0,1:T(8,128)S(1)}, u32[]{:S(2)}) copy-start(f32[2048,896]{0,1:T(8,128)S(1)} %broadcast_in_dim.74) | copy-start | bytes 22020100
  423.4 17.7 %copy-start.12 = (bf16[2048,1920]{0,1:T(8,128)(2,1)S(1)}, bf16[2048,1920]{0,1:T(8,128)(2,1)}, u32[]{:S(2)}) copy-start(bf16[2048,1920]{0,1:T(8,128)(2,1)} %get-tuple-element.129) | copy-start | bytes 23592964
  441.1 14.8 %copy-start.55 = (bf16[1408]{0:T(1024)(128)(2,1)S(1)}, bf16[1408]{0:T(1024)(128)(2,1)}, u32[]{:S(2)}) copy-start(bf16[1408]{0:T(1024)(128)(2,1)} %pad.23.clone) | copy-start | bytes 8452
  464.0 125.8 %reduce-scatter.9.cloned.1.call-start = ((), (), s32[]{:S(2)}) async-start(), calls=%async_computation.9 | async-start | bytes 5898240 | tf_op jit(solution)/shard_map/reduce_scatter | solution.py:88
  486.3 45.4 %copy-start.8 = (f32[256,1280]{0,1:T(8,128)S(1)}, f32[256,1280]{0,1:T(8,128)}, u32[]{:S(2)}) copy-start(f32[256,1280]{0,1:T(8,128)} %copy-done.7) | copy-start | bytes 3932164
  486.3 45.4 %copy-start.52 = (f32[1280]{0:T(1024)S(1)}, f32[1280]{0:T(1024)}, u32[]{:S(2)}) copy-start(f32[1280]{0:T(1024)} %copy-done.51) | copy-start | bytes 15364
  486.3 45.4 %copy-start.57 = (f32[256]{0:T(256)S(1)}, f32[256]{0:T(256)}, u32[]{:S(2)}) copy-start(f32[256]{0:T(256)} %copy-done.56) | copy-start | bytes 3076
  486.3 103.5 %copy-start.66 = (f32[256]{0:T(256)S(1)}, f32[256]{0:T(256)}, u32[]{:S(2)}) copy-start(f32[256]{0:T(256)} %get-tuple-element.169) | copy-start | bytes 3076
  486.4 431.3 %reduce-scatter.15.cloned.1.call-start = ((), (), s32[]{:S(2)}) async-start(), calls=%async_computation.13 | async-start | bytes 14745600
  595.9 13.5 %slice-start = ((s8[13107200]{0:T(1024)(128)(4,1)}), s8[524288]{0:T(1024)(128)(4,1)S(1)}, s32[]{:S(2)}) async-start(s8[13107200]{0:T(1024)(128)(4,1)} %bitcast.92), calls=%async_computation.15 | async-start | bytes 1048576
  597.2 12.2 slice-start.1
  597.2 12.2 slice-start.2
  597.3 13.9 %slice-start.3 = ((s8[13107200]{0:T(1024)(128)(4,1)}), s8[4194304]{0:T(1024)(128)(4,1)S(1)}, s32[]{:S(2)}) async-start(s8[13107200]{0:T(1024)(128)(4,1)} %bitcast.92), calls=%async_computation.18 | async-start | bytes 8388608
  614.9 6.6 copy-start.14
  614.9 6.6 copy-start.26
  732.9 182.4 %all-to-all-start.1 = ((bf16[8,160,224]{2,1,0:T(8,128)(2,1)}), bf16[8,160,224]{2,1,0:T(8,128)(2,1)S(1)}, u32[]{:S(2)}, u32[]{:S(2)}) async-start(bf16[8,160,224]{2,1,0:T(8,128)(2,1)} %bitcast.30), calls=%async_computation.3 | async-start | bytes 1310720 | tf_op jit(solution)/shard_map/all_to_all | solution.py:316
  736.5 202.5 %reduce-scatter.13.cloned.1.call-start = ((), (), s32[]{:S(2)}) async-start(), calls=%async_computation.12 | async-start | bytes 368640
  736.5 20.1 %slice-start.4 = ((s8[7864320]{0:T(1024)(128)(4,1)}), s8[4194304]{0:T(1024)(128)(4,1)S(1)}, s32[]{:S(2)}) async-start(s8[7864320]{0:T(1024)(128)(4,1)} %bitcast.97), calls=%async_computation.19 | async-start | bytes 8388608
  736.5 20.0 %slice-start.6 = ((s8[5242880]{0:T(1024)(128)(4,1)}), s8[4194304]{0:T(1024)(128)(4,1)S(1)}, s32[]{:S(2)}) async-start(s8[5242880]{0:T(1024)(128)(4,1)} %bitcast.103), calls=%async_computation.21 | async-start | bytes 8388608
  746.7 9.9 slice-start.5
  746.7 9.9 slice-start.7
  756.6 6.9 copy-start.22
  779.4 16.3 %collective-permute-start.4 = (bf16[256,1280]{0,1:T(8,128)(2,1)S(1)}, bf16[256,1280]{0,1:T(8,128)(2,1)S(1)}, u32[]{:S(2)}, u32[]{:S(2)}) collective-permute-start(bf16[256,1280]{0,1:T(8,128)(2,1)S(1)} %get-tuple-element.139), channel_id=1, source_target_pairs={{1,0},{2,1},{3,2},{4,3},{5,4},{6,5},{7,6},{8,7},{9,8},{10,9},{11,1... | collective-permute-start | bytes 1966088 | tf_op jit(solution)/shard_map/ppermute | solution.py:25
  780.7 60.8 %collective-permute-start.5 = (bf16[256,1280]{0,1:T(8,128)(2,1)S(1)}, bf16[256,1280]{0,1:T(8,128)(2,1)S(1)}, u32[]{:S(2)}, u32[]{:S(2)}) collective-permute-start(bf16[256,1280]{0,1:T(8,128)(2,1)S(1)} %get-tuple-element.142), channel_id=1, source_target_pairs={{2,0},{3,1},{4,2},{5,3},{6,4},{7,5},{8,6},{9,7},{10,8},{11,9},{12,... | collective-permute-start | bytes 1966088 | tf_op jit(solution)/shard_map/ppermute | solution.py:25
  782.0 60.9 %collective-permute-start.6 = (bf16[256,1280]{0,1:T(8,128)(2,1)S(1)}, bf16[256,1280]{0,1:T(8,128)(2,1)S(1)}, u32[]{:S(2)}, u32[]{:S(2)}) collective-permute-start(bf16[256,1280]{0,1:T(8,128)(2,1)S(1)} %get-tuple-element.141), channel_id=1, source_target_pairs={{3,0},{4,1},{5,2},{6,3},{7,4},{8,5},{9,6},{10,7},{11,8},{12,9},{13... | collective-permute-start | bytes 1966088 | tf_op jit(solution)/shard_map/ppermute | solution.py:25
  783.3 8.7 copy-start.30
  783.3 8.7 copy-start.31
  783.3 121.2 %collective-permute-start.7 = (bf16[256,1280]{0,1:T(8,128)(2,1)S(1)}, bf16[256,1280]{0,1:T(8,128)(2,1)S(1)}, u32[]{:S(2)}, u32[]{:S(2)}) collective-permute-start(bf16[256,1280]{0,1:T(8,128)(2,1)S(1)} %get-tuple-element.140), channel_id=1, source_target_pairs={{4,0},{5,1},{6,2},{7,3},{8,4},{9,5},{10,6},{11,7},{12,8},{13,9},{1... | collective-permute-start | bytes 1966088 | tf_op jit(solution)/shard_map/ppermute | solution.py:25
  910.3 354.6 %all-reduce.3.cloned.1.call-start = ((), (), s32[]{:S(2)}) async-start(), calls=%async_computation.14 | async-start | bytes 34488320 | tf_op jit(solution)/shard_map/psum | solution.py:432
  1264.9 7.2 copy-start.20
  1264.9 11.4 slice-start.10
  1282.6 7.8 copy-start.46
  1282.6 8.6 copy-start.45
  1282.6 9.5 copy-start.44
  (39 other events, 101.7 us)
Sparse Core Ops, SparseCore 0:
  11.7 105.0 all-gather.4
  118.9 91.2 all-gather.6
  211.9 54.4 all-gather.10
  268.4 58.2 all-gather.8
  464.1 65.1 reduce-scatter.10
  531.5 58.2 reduce-scatter.8
  689.6 186.1 reduce-scatter.14
  910.5 28.4 reduce-scatter.12
  945.6 319.3 all-reduce.2
